TPU v7x, 32 devices: a whole 2x2x4 slice. The times are simulated.
32 devices in a mesh: rows: 8 (over z, y), cols: 4 (over x, core).
Axes of the slice: x: 2, y: 2, z: 4, core: 2. Of those that a mesh axis runs over, the one named last changes fastest.
Arguments:
- hblocks: float32 [64, 24, 128, 128], P('rows'), may hold values from -0.0546875 to 0.0546875
- col_index: int32 [64, 24], P('rows'), may hold values from 0 to 63, as said below
- right_side: float32 [64, 64, 128], P('rows', 'cols'), may hold values from -12 to 12
- center: float32 [1], replicated, may hold values from -0.5 to 0.5
- shifts: float32 [8], replicated, may hold values from 0.05 to 2
- filter_weights: float32 [8], replicated, may hold values from 0.03 to 0.3
Outputs:
- filtered: float32 [64, 64, 128], P('rows', 'cols')
- gram_matrix: float32 [64, 64], P(None, 'cols')
- ritz_matrix: float32 [64, 64], P(None, 'cols')
Inputs may be any that keep to these rules, and one draw needn't show every extreme that they name: `col_index`: block rows are held 8 to a device of rows, in order. In block row i the first 8 column indices are the 8 block rows of the device that holds i, each once. Every other column index of a block row lies on another device of rows; for each pair of distinct devices, the block rows of the one that are named by the block rows of the other are exactly 2 distinct ones.
All inputs are finite; a program needn't handle non-finite values.
Results may differ from a plain program's by a relative error of at most 0.0001.
Values sent between devices are 32-bit elements; how exact they have to be, the bound alone decides.
A program may use at most 64 MiB of HBM per device.

v0:
```python
import jax
import jax.numpy as jnp
from jax import lax
from jax.sharding import PartitionSpec as P

CAP = 2
ITERS = 2


exact_mode = lax.Precision.HIGHEST


def column_dot(first_arr, second_arr):
    return jnp.sum(first_arr * second_arr, axis=(0, 2))


def ordered_lists(need_mask, slot_width):
    ranks = jnp.cumsum(need_mask, axis=1)
    positions = lax.broadcasted_iota(jnp.int32, need_mask.shape, 1)
    columns_out = []
    for slot in range(slot_width):
        hit = (need_mask > 0) & (ranks == slot + 1)
        columns_out.append(jnp.sum(jnp.where(hit, positions, 0), axis=1))
    lists = jnp.stack(columns_out, axis=1)
    live = jnp.sum(need_mask, axis=1, keepdims=True) > 0
    return jnp.where(live, lists, -1)


def shards(hblocks, col_index, right_side, center, shifts, filter_weights):
    block_rows = hblocks.shape[0]
    block_width = hblocks.shape[2]
    local_vecs = right_side.shape[1]
    pole_count = shifts.shape[0]
    peer_count = lax.axis_size("rows")
    slot_width = CAP
    device_index = lax.axis_index("rows")
    own_cols = col_index[:, :block_rows] - device_index * block_rows
    far_cols = col_index[:, block_rows:].reshape(-1)
    near_blocks = hblocks[:, :block_rows]
    far_blocks = hblocks[:, block_rows:]
    every_key = jnp.arange(peer_count * block_rows, dtype=jnp.int32)
    need_mask = (
        jnp.any(far_cols[:, None] == every_key[None, :], axis=0)
        .astype(jnp.int32)
        .reshape(peer_count, block_rows)
    )
    incoming_mask = lax.all_to_all(need_mask, "rows", split_axis=0, concat_axis=0, tiled=True)
    send_lists = ordered_lists(incoming_mask, slot_width)
    my_lists = ordered_lists(need_mask, slot_width)
    owners = lax.broadcasted_iota(jnp.int32, my_lists.shape, 0)
    slot_keys = jnp.where(my_lists >= 0, owners * block_rows + my_lists, -1).reshape(-1)
    slot_total = slot_keys.shape[0]
    matches = far_cols[:, None] == slot_keys[None, :]
    picker = matches.astype(jnp.float32)
    slot_numbers = lax.broadcasted_iota(jnp.int32, matches.shape, 1)
    slot_of_ref = jnp.sum(jnp.where(matches, slot_numbers, 0), axis=1)
    row_numbers = jnp.arange(block_rows, dtype=jnp.int32)[:, None]
    spread = (send_lists.reshape(-1)[None, :] == row_numbers).astype(jnp.float32)
    own_spread = (own_cols.reshape(-1)[None, :] == row_numbers).astype(jnp.float32)
    send_index = jnp.maximum(send_lists, 0)
    send_live = (send_lists >= 0)[:, :, None, None]

    def apply_h(vector):
        picked = vector[send_index]
        outgoing = jnp.where(send_live, picked, jnp.zeros_like(picked))
        arrived = lax.all_to_all(outgoing, "rows", split_axis=0, concat_axis=0, tiled=True).reshape(
            slot_total, local_vecs, block_width
        )
        far_vec = arrived[slot_of_ref]
        far_vec = far_vec.reshape(block_rows, -1, local_vecs, block_width)
        near_vec = vector[own_cols]
        result = jnp.einsum("ikab,ikvb->iva", near_blocks, near_vec, precision=exact_mode)
        result = result + jnp.einsum("ikab,ikvb->iva", far_blocks, far_vec, precision=exact_mode)
        near_terms = jnp.einsum(
            "ikab,iva->ikvb", near_blocks, vector, precision=exact_mode
        ).reshape(block_rows * block_rows, -1)
        result = result + jnp.dot(own_spread, near_terms, precision=exact_mode).reshape(
            vector.shape
        )
        far_terms = jnp.einsum("ikab,iva->ikvb", far_blocks, vector, precision=exact_mode).reshape(
            far_cols.shape[0], -1
        )
        slot_sums = jnp.dot(picker.T, far_terms, precision=exact_mode).reshape(
            peer_count, slot_width, local_vecs, block_width
        )
        returned = lax.all_to_all(
            slot_sums, "rows", split_axis=0, concat_axis=0, tiled=True
        ).reshape(slot_total, -1)
        return result + jnp.dot(spread, returned, precision=exact_mode).reshape(vector.shape)

    center_value = center[0]
    base_shift = jnp.min(shifts)
    delta_shift = (shifts - base_shift)[:, None]
    residual = right_side
    solutions = jnp.zeros((pole_count,) + right_side.shape, jnp.float32)
    shifted_dirs = jnp.broadcast_to(right_side, solutions.shape)
    zeta_prev = jnp.ones((pole_count, local_vecs), jnp.float32)
    zeta_now = jnp.ones((pole_count, local_vecs), jnp.float32)
    alpha_prev = jnp.ones((local_vecs,), jnp.float32)
    beta_prev = jnp.zeros((local_vecs,), jnp.float32)

    def squares(vector):
        return lax.psum(column_dot(vector, vector), "rows")

    direction = right_side
    res_norm = squares(residual)
    for iteration in range(ITERS):
        shifted = apply_h(direction) - center_value * direction
        op_image = apply_h(shifted) - center_value * shifted + base_shift * direction
        alpha_now = res_norm / lax.psum(column_dot(direction, op_image), "rows")
        solution_solutions = solutions
        zeta_next = (
            zeta_now
            * zeta_prev
            * alpha_prev
            / (
                alpha_now * beta_prev * (zeta_prev - zeta_now)
                + zeta_prev * alpha_prev * (1.0 + delta_shift * alpha_now)
            )
        )
        zeta_ratio = zeta_next / zeta_now
        solution_solutions = (
            solution_solutions + (alpha_now * zeta_ratio)[:, None, :, None] * shifted_dirs
        )
        solutions, zeta_next, zeta_ratio = (solution_solutions, zeta_next, zeta_ratio)
        residual = residual - alpha_now[None, :, None] * op_image
        if iteration + 1 < ITERS:
            norm_next = squares(residual)
            beta_now = norm_next / res_norm
            direction = residual + beta_now[None, :, None] * direction
            shifted_dirs = (
                zeta_next[:, None, :, None] * residual[None]
                + (beta_now * zeta_ratio * zeta_ratio)[:, None, :, None] * shifted_dirs
            )
            zeta_prev, zeta_now, alpha_prev, beta_prev, res_norm = (
                zeta_now,
                zeta_next,
                alpha_now,
                beta_now,
                norm_next,
            )
    filtered = jnp.sum(filter_weights[:, None, None, None] * solutions, axis=0)
    applied = apply_h(filtered)
    column_piece = lax.all_gather(filtered, "cols", axis=1, tiled=True)
    correlation = jnp.einsum("iae,ibe->ab", column_piece, filtered, precision=exact_mode)
    projected = jnp.einsum("iae,ibe->ab", column_piece, applied, precision=exact_mode)
    partial_gram = jnp.stack([correlation, projected])
    summed = lax.psum(partial_gram, "rows")
    row_total = peer_count * block_rows * block_width
    return (filtered, summed[0] / row_total, summed[1] / row_total)


def solution(mesh):
    placed = (P("rows", None, None, None), P("rows", None), P("rows", "cols", None), P(), P(), P())
    return jax.shard_map(
        shards,
        mesh=mesh,
        in_specs=placed,
        out_specs=(P("rows", "cols", None), P(None, "cols"), P(None, "cols")),
        check_vma=False,
    )
```

profile of v0, /device:TPU:0, one launch (start us, length us, event | category | flops | bytes accessed | tf_op | source)
XLA Modules:
  0.0 356.9 jit_solution(17650875940720116990)
XLA Ops:
  0.7 0.8 slice.20
  2.4 7.3 %all-to-all-start = ((s32[8,1,8]{2,1,0:T(1,128)}), s32[8,1,8]{2,1,0:T(1,128)S(1)}, u32[]{:S(2)}, u32[]{:S(2)}) async-start(s32[8,1,8]{2,1,0:T(1,128)} %bitcast.3), calls=%async_computation | async-start | bytes 8192 | tf_op jit(solution)/shard_map/all_to_all | solution.py:47
  10.0 6.4 %fusion.16 = f32[8,16,16,128]{3,1,2,0:T(8,128)S(1)} fusion(f32[8,24,128,128]{3,2,1,0:T(8,128)} %param.6, f32[8,16,128]{2,1,0:T(8,128)} %param.8), kind=kOutput, calls=%fused_computation.31 | convolution fusion | flops 402653184 | bytes 9502720 | tf_op jit(solution)/shard_map/ikab,iva->ikvb/dot_general | solution.py:80
  16.4 3.9 %fusion.40 = f32[8,8,16,128]{3,2,1,0:T(8,128)S(1)} fusion(f32[8,24,128,128]{3,2,1,0:T(8,128)} %param.6, f32[8,16,128]{2,1,0:T(8,128)} %param.8), kind=kOutput, calls=%fused_computation.55 | convolution fusion | flops 201326592 | bytes 4784128 | tf_op jit(solution)/shard_map/ikab,iva->ikvb/dot_general | solution.py:74
  22.8 5.3 %fusion.55 = f32[8,16,128]{2,1,0:T(8,128)S(1)} fusion(f32[8,8,16,128]{3,2,1,0:T(8,128)S(1)} %bitcast.449, f32[8,24,128,128]{3,2,1,0:T(8,128)} %param.6), kind=kOutput, calls=%fused_computation.60 | convolution fusion | flops 201326592 | bytes 4784128 | tf_op jit(solution)/shard_map/ikab,ikvb->iva/dot_general | solution.py:72
  30.0 6.0 %all-to-all-start.2 = ((f32[8,2,16,128]{3,2,1,0:T(8,128)}), f32[8,2,16,128]{3,2,1,0:T(8,128)S(1)}, u32[]{:S(2)}, u32[]{:S(2)}) async-start(f32[8,2,16,128]{3,2,1,0:T(8,128)} %copy.169), calls=%async_computation.2 | async-start | bytes 262144 | tf_op jit(solution)/shard_map/all_to_all | solution.py:86
  38.2 5.2 %all-to-all-done.2 = f32[8,2,16,128]{3,2,1,0:T(8,128)S(1)} async-done(((f32[8,2,16,128]{3,2,1,0:T(8,128)}), f32[8,2,16,128]{3,2,1,0:T(8,128)S(1)}, u32[]{:S(2)}, u32[]{:S(2)}) %all-to-all-start.2) | async-done | bytes 131104 | tf_op jit(solution)/shard_map/all_to_all | solution.py:86
  43.3 3.9 %all-to-all-start.1 = ((f32[8,2,16,128]{3,2,1,0:T(8,128)}), f32[8,2,16,128]{3,2,1,0:T(8,128)S(1)}, u32[]{:S(2)}, u32[]{:S(2)}) async-start(f32[8,2,16,128]{3,2,1,0:T(8,128)} %broadcast_select_fusion.4), calls=%async_computation.1 | async-start | bytes 262144 | tf_op jit(solution)/shard_map/all_to_all | solution.py:66
  48.2 6.3 %all-to-all-done.1 = f32[8,2,16,128]{3,2,1,0:T(8,128)S(1)} async-done(((f32[8,2,16,128]{3,2,1,0:T(8,128)}), f32[8,2,16,128]{3,2,1,0:T(8,128)S(1)}, u32[]{:S(2)}, u32[]{:S(2)}) %all-to-all-start.1) | async-done | bytes 131104 | tf_op jit(solution)/shard_map/all_to_all | solution.py:66
  54.5 0.8 gather_fusion.2
  55.3 9.3 %fusion.148 = f32[8,16,128]{2,1,0:T(8,128)S(1)} fusion(f32[8,16,128]{2,1,0:T(8,128)S(1)} %fusion.55, f32[8,16,16,128]{3,2,1,0:T(8,128)S(1)} %bitcast.426, f32[8,24,128,128]{3,2,1,0:T(8,128)} %param.6, f32[8,16,128]{2,0,1:T(8,128)S(1)} %fusion.181, f32[8,16,128]{2,0,1:T(8,128)S(1)} %fusion.166, f32[8,16,128]{2,1,0:T(8,128)S(1)} %copy-done, f32[]{:T(128)} %bitcast.416), kind=kOutput, calls=%fused_computation.91 | convolution fusion | flops 402735104 | bytes 9765376 | tf_op jit(solution)/shard_map/ikab,ikvb->iva/dot_general | solution.py:73
  64.6 6.4 %fusion.12 = f32[8,16,16,128]{3,1,2,0:T(8,128)S(1)} fusion(f32[8,24,128,128]{3,2,1,0:T(8,128)} %param.6, f32[8,16,128]{2,1,0:T(8,128)S(1)} %fusion.148), kind=kOutput, calls=%fused_computation.27 | convolution fusion | flops 402653184 | bytes 9502720 | tf_op jit(solution)/shard_map/ikab,iva->ikvb/dot_general | solution.py:80
  72.2 3.8 %fusion.43 = f32[8,8,16,128]{3,2,1,0:T(8,128)S(1)} fusion(f32[8,24,128,128]{3,2,1,0:T(8,128)} %param.6, f32[8,16,128]{2,1,0:T(8,128)S(1)} %fusion.148), kind=kOutput, calls=%fused_computation.56 | convolution fusion | flops 201326592 | bytes 4784128 | tf_op jit(solution)/shard_map/ikab,iva->ikvb/dot_general | solution.py:74
  78.0 3.4 all-to-all-start.4
  81.4 5.3 %fusion.58 = f32[8,16,128]{2,1,0:T(8,128)S(1)} fusion(f32[8,8,16,128]{3,2,1,0:T(8,128)S(1)} %bitcast.446, f32[8,24,128,128]{3,2,1,0:T(8,128)} %param.6), kind=kOutput, calls=%fused_computation.61 | convolution fusion | flops 201326592 | bytes 4784128 | tf_op jit(solution)/shard_map/ikab,ikvb->iva/dot_general | solution.py:72
  87.4 1.2 all-to-all-done.4
  88.6 4.9 %all-to-all-start.3 = ((f32[8,2,16,128]{3,2,1,0:T(8,128)}), f32[8,2,16,128]{3,2,1,0:T(8,128)S(1)}, u32[]{:S(2)}, u32[]{:S(2)}) async-start(f32[8,2,16,128]{3,2,1,0:T(8,128)} %broadcast_select_fusion.3), calls=%async_computation.3 | async-start | bytes 262144 | tf_op jit(solution)/shard_map/all_to_all | solution.py:66
  94.2 6.7 %all-to-all-done.3 = f32[8,2,16,128]{3,2,1,0:T(8,128)S(1)} async-done(((f32[8,2,16,128]{3,2,1,0:T(8,128)}), f32[8,2,16,128]{3,2,1,0:T(8,128)S(1)}, u32[]{:S(2)}, u32[]{:S(2)}) %all-to-all-start.3) | async-done | bytes 131104 | tf_op jit(solution)/shard_map/all_to_all | solution.py:66
  100.8 0.8 gather_fusion.5
  101.6 10.1 %multiply_reduce_fusion.2 = (f32[16]{0:T(128)S(1)}, f32[16]{0:T(128)S(1)}, f32[8,16,128]{2,1,0:T(8,128)S(1)}) fusion(f32[8,16,128]{2,1,0:T(8,128)S(1)} %copy-done, f32[]{:T(128)} %reduce_min.9, f32[8,16,128]{2,1,0:T(8,128)S(1)} %fusion.148, f32[]{:T(128)} %bitcast.419, f32[8,16,128]{2,0,1:T(8,128)S(1)} %fusion.178, f32[8,16,128]{2,0,1:T(8,128)S(1)} %fusion.163, ...), kind=kOutput, calls=%fused_computation.154 | convolution fusion | flops 402833376 | bytes 9831552 | tf_op jit(solution)/shard_map/ikab,ikvb->iva/dot_general | solution.py:73
  111.7 18.2 %all-reduce = (f32[16]{0:T(128)S(1)}, f32[16]{0:T(128)S(1)}) all-reduce(f32[16]{0:T(128)S(1)} %get-tuple-element.4, f32[16]{0:T(128)S(1)} %get-tuple-element.3), channel_id=1, replica_groups=mesh['rows'=8,'cols'=4] {'rows'}, use_global_device_ids=true, to_apply=%region_1.0 | all-reduce | flops 32 | bytes 256 | tf_op jit(solution)/shard_map/psum | solution.py:103
  131.0 18.1 %psum.37 = f32[16]{0:T(128)S(1)} all-reduce(f32[16]{0:T(128)S(1)} %get-tuple-element.15), channel_id=1, replica_groups=mesh['rows'=8,'cols'=4] {'rows'}, use_global_device_ids=true, to_apply=%region_16.17 | all-reduce | flops 16 | bytes 128 | tf_op jit(solution)/shard_map/psum | solution.py:103
  149.6 6.4 %fusion.8 = f32[8,16,16,128]{3,1,2,0:T(8,128)S(1)} fusion(f32[8,24,128,128]{3,2,1,0:T(8,128)} %param.6, f32[8,16,128]{2,1,0:T(8,128)S(1)} %multiply_add_fusion), kind=kOutput, calls=%fused_computation.23 | convolution fusion | flops 402653184 | bytes 9502720 | tf_op jit(solution)/shard_map/ikab,iva->ikvb/dot_general | solution.py:80
  156.6 3.8 %fusion.46 = f32[8,8,16,128]{3,2,1,0:T(8,128)S(1)} fusion(f32[8,24,128,128]{3,2,1,0:T(8,128)} %param.6, f32[8,16,128]{2,1,0:T(8,128)S(1)} %multiply_add_fusion), kind=kOutput, calls=%fused_computation.57 | convolution fusion | flops 201326592 | bytes 4784128 | tf_op jit(solution)/shard_map/ikab,iva->ikvb/dot_general | solution.py:74
  163.0 3.4 all-to-all-start.6
  166.4 5.3 %fusion.61 = f32[8,16,128]{2,1,0:T(8,128)S(1)} fusion(f32[8,8,16,128]{3,2,1,0:T(8,128)S(1)} %bitcast.447, f32[8,24,128,128]{3,2,1,0:T(8,128)} %param.6), kind=kOutput, calls=%fused_computation.62 | convolution fusion | flops 201326592 | bytes 4784128 | tf_op jit(solution)/shard_map/ikab,ikvb->iva/dot_general | solution.py:72
  172.4 1.2 all-to-all-done.6
  173.7 4.9 %all-to-all-start.5 = ((f32[8,2,16,128]{3,2,1,0:T(8,128)}), f32[8,2,16,128]{3,2,1,0:T(8,128)S(1)}, u32[]{:S(2)}, u32[]{:S(2)}) async-start(f32[8,2,16,128]{3,2,1,0:T(8,128)} %broadcast_select_fusion.2), calls=%async_computation.5 | async-start | bytes 262144 | tf_op jit(solution)/shard_map/all_to_all | solution.py:66
  178.6 1.0 fusion.160
  179.6 0.9 fusion.175
  180.5 5.4 %all-to-all-done.5 = f32[8,2,16,128]{3,2,1,0:T(8,128)S(1)} async-done(((f32[8,2,16,128]{3,2,1,0:T(8,128)}), f32[8,2,16,128]{3,2,1,0:T(8,128)S(1)}, u32[]{:S(2)}, u32[]{:S(2)}) %all-to-all-start.5) | async-done | bytes 131104 | tf_op jit(solution)/shard_map/all_to_all | solution.py:66
  185.9 0.9 gather_fusion.8
  186.8 9.3 %fusion.121 = f32[8,16,128]{2,1,0:T(8,128)S(1)} fusion(f32[8,16,128]{2,1,0:T(8,128)S(1)} %fusion.61, f32[8,16,16,128]{3,2,1,0:T(8,128)S(1)} %bitcast.427, f32[8,24,128,128]{3,2,1,0:T(8,128)} %param.6, f32[8,16,128]{2,0,1:T(8,128)S(1)} %fusion.175, f32[8,16,128]{2,0,1:T(8,128)S(1)} %fusion.160, f32[8,16,128]{2,1,0:T(8,128)S(1)} %multiply_add_fusion, ...), kind=kOutput, calls=%fused_computation.82 | convolution fusion | flops 402735104 | bytes 9765376 | tf_op jit(solution)/shard_map/ikab,ikvb->iva/dot_general | solution.py:73
  196.1 6.4 %fusion.4 = f32[8,16,16,128]{3,1,2,0:T(8,128)S(1)} fusion(f32[8,24,128,128]{3,2,1,0:T(8,128)} %param.6, f32[8,16,128]{2,1,0:T(8,128)S(1)} %fusion.121), kind=kOutput, calls=%fused_computation.19 | convolution fusion | flops 402653184 | bytes 9502720 | tf_op jit(solution)/shard_map/ikab,iva->ikvb/dot_general | solution.py:80
  203.1 3.8 %fusion.49 = f32[8,8,16,128]{3,2,1,0:T(8,128)S(1)} fusion(f32[8,24,128,128]{3,2,1,0:T(8,128)} %param.6, f32[8,16,128]{2,1,0:T(8,128)S(1)} %fusion.121), kind=kOutput, calls=%fused_computation.58 | convolution fusion | flops 201326592 | bytes 4784128 | tf_op jit(solution)/shard_map/ikab,iva->ikvb/dot_general | solution.py:74
  208.2 1.3 fusion.199
  210.2 3.4 all-to-all-start.8
  213.6 5.3 %fusion.64 = f32[8,16,128]{2,1,0:T(8,128)S(1)} fusion(f32[8,8,16,128]{3,2,1,0:T(8,128)S(1)} %bitcast.448, f32[8,24,128,128]{3,2,1,0:T(8,128)} %param.6), kind=kOutput, calls=%fused_computation.63 | convolution fusion | flops 201326592 | bytes 4784128 | tf_op jit(solution)/shard_map/ikab,ikvb->iva/dot_general | solution.py:72
  219.6 1.2 all-to-all-done.8
  220.8 5.0 %all-to-all-start.7 = ((f32[8,2,16,128]{3,2,1,0:T(8,128)}), f32[8,2,16,128]{3,2,1,0:T(8,128)S(1)}, u32[]{:S(2)}, u32[]{:S(2)}) async-start(f32[8,2,16,128]{3,2,1,0:T(8,128)} %broadcast_select_fusion.1), calls=%async_computation.7 | async-start | bytes 262144 | tf_op jit(solution)/shard_map/all_to_all | solution.py:66
  225.8 1.0 fusion.157
  226.8 0.9 fusion.172
  227.7 5.4 %all-to-all-done.7 = f32[8,2,16,128]{3,2,1,0:T(8,128)S(1)} async-done(((f32[8,2,16,128]{3,2,1,0:T(8,128)}), f32[8,2,16,128]{3,2,1,0:T(8,128)S(1)}, u32[]{:S(2)}, u32[]{:S(2)}) %all-to-all-start.7) | async-done | bytes 131104 | tf_op jit(solution)/shard_map/all_to_all | solution.py:66
  233.1 0.9 gather_fusion.11
  234.0 10.1 %fusion.151 = f32[16]{0:T(128)S(1)} fusion(f32[8,16,128]{2,1,0:T(8,128)S(1)} %multiply_add_fusion, f32[8,16,128]{2,1,0:T(8,128)S(1)} %fusion.64, f32[8,16,16,128]{3,2,1,0:T(8,128)S(1)} %bitcast.444, f32[8,24,128,128]{3,2,1,0:T(8,128)} %param.6, f32[8,16,128]{2,0,1:T(8,128)S(1)} %fusion.172, f32[8,16,128]{2,0,1:T(8,128)S(1)} %fusion.157, ...), kind=kOutput, calls=%fused_computation.92 | convolution fusion | flops 402800640 | bytes 9765952 | tf_op jit(solution)/shard_map/ikab,ikvb->iva/dot_general | solution.py:73
  244.1 1.3 broadcast_subtract_fusion
  245.4 18.2 %psum.38 = f32[16]{0:T(128)S(1)} all-reduce(f32[16]{0:T(128)S(1)} %fusion.151), channel_id=1, replica_groups=mesh['rows'=8,'cols'=4] {'rows'}, use_global_device_ids=true, to_apply=%region_18.19 | all-reduce | flops 16 | bytes 128 | tf_op jit(solution)/shard_map/psum | solution.py:110
  264.3 0.8 broadcast_multiply_fusion
  265.0 0.9 multiply_reduce_fusion
  266.0 5.8 %all_gather.3 = f32[8,64,128]{2,1,0:T(8,128)S(1)} all-gather(f32[8,16,128]{2,1,0:T(8,128)S(1)} %multiply_reduce_fusion), channel_id=1, replica_groups=mesh['rows'=8,'cols'=4] {'cols'}, dimensions={1}, use_global_device_ids=true | all-gather | bytes 327680 | tf_op jit(solution)/shard_map/all_gather | solution.py:144
  271.7 6.4 %fusion = f32[8,16,16,128]{3,1,2,0:T(8,128)S(1)} fusion(f32[8,24,128,128]{3,2,1,0:T(8,128)} %param.6, f32[8,16,128]{2,1,0:T(8,128)S(1)} %multiply_reduce_fusion), kind=kOutput, calls=%fused_computation.15 | convolution fusion | flops 402653184 | bytes 9502720 | tf_op jit(solution)/shard_map/ikab,iva->ikvb/dot_general | solution.py:80
  278.1 1.2 gather_fusion.13
  279.9 3.8 %fusion.52 = f32[8,8,16,128]{3,2,1,0:T(8,128)S(1)} fusion(f32[8,24,128,128]{3,2,1,0:T(8,128)} %param.6, f32[8,16,128]{2,1,0:T(8,128)S(1)} %multiply_reduce_fusion), kind=kOutput, calls=%fused_computation.59 | convolution fusion | flops 201326592 | bytes 4784128 | tf_op jit(solution)/shard_map/ikab,iva->ikvb/dot_general | solution.py:74
  284.5 1.3 fusion.197
  286.4 3.4 all-to-all-start.10
  289.8 5.3 %fusion.67 = f32[8,16,128]{2,1,0:T(8,128)S(1)} fusion(f32[8,8,16,128]{3,2,1,0:T(8,128)S(1)} %bitcast.445, f32[8,24,128,128]{3,2,1,0:T(8,128)} %param.6), kind=kOutput, calls=%fused_computation.64 | convolution fusion | flops 201326592 | bytes 4784128 | tf_op jit(solution)/shard_map/ikab,ikvb->iva/dot_general | solution.py:72
  295.1 1.0 fusion.154
  296.1 1.6 broadcast_select_fusion
  297.8 6.4 %all-to-all-start.9 = ((f32[8,2,16,128]{3,2,1,0:T(8,128)}), f32[8,2,16,128]{3,2,1,0:T(8,128)S(1)}, u32[]{:S(2)}, u32[]{:S(2)}) async-start(f32[8,2,16,128]{3,2,1,0:T(8,128)} %broadcast_select_fusion), calls=%async_computation.9 | async-start | bytes 262144 | tf_op jit(solution)/shard_map/all_to_all | solution.py:66
  304.5 0.9 fusion.169
  305.4 6.1 %all-to-all-done.9 = f32[8,2,16,128]{3,2,1,0:T(8,128)S(1)} async-done(((f32[8,2,16,128]{3,2,1,0:T(8,128)}), f32[8,2,16,128]{3,2,1,0:T(8,128)S(1)}, u32[]{:S(2)}, u32[]{:S(2)}) %all-to-all-start.9) | async-done | bytes 131104 | tf_op jit(solution)/shard_map/all_to_all | solution.py:66
  311.5 0.9 gather_fusion.14
  312.4 9.3 %fusion.91 = f32[8,16,128]{2,1,0:T(8,128)S(1)} fusion(f32[8,16,128]{2,1,0:T(8,128)S(1)} %fusion.67, f32[8,16,16,128]{3,2,1,0:T(8,128)S(1)} %bitcast.425, f32[8,24,128,128]{3,2,1,0:T(8,128)} %param.6, f32[8,16,128]{2,0,1:T(8,128)S(1)} %fusion.169, f32[8,16,128]{2,0,1:T(8,128)S(1)} %fusion.154), kind=kOutput, calls=%fused_computation.72 | convolution fusion | flops 402702336 | bytes 9699328 | tf_op jit(solution)/shard_map/ikab,ikvb->iva/dot_general | solution.py:73
  322.0 34.1 %psum.39 = f32[2,64,16]{1,2,0:T(8,128)S(1)} all-reduce(f32[2,64,16]{1,2,0:T(8,128)S(1)} %pad_maximum_fusion), channel_id=1, replica_groups=mesh['rows'=8,'cols'=4] {'rows'}, use_global_device_ids=true, to_apply=%region_20.21 | all-reduce | flops 2048 | bytes 16384 | tf_op jit(solution)/shard_map/psum | solution.py:148
  (103 shorter events, 25.1 us)
Async XLA Ops:
  0.6 21.4 %copy-start.6 = (s32[8,24]{1,0:T(8,128)S(1)}, s32[8,24]{1,0:T(8,128)}, u32[]{:S(2)}) copy-start(s32[8,24]{1,0:T(8,128)} %param.7) | copy-start | bytes 2308
  0.6 21.5 %copy-start = (f32[8,16,128]{2,1,0:T(8,128)S(1)}, f32[8,16,128]{2,1,0:T(8,128)}, u32[]{:S(2)}) copy-start(f32[8,16,128]{2,1,0:T(8,128)} %param.8) | copy-start | bytes 196612
  1.5 110.2 %copy-start.2 = (s32[128]{0:T(128)}, s32[128]{0:T(128)S(1)}, u32[]{:S(2)}) copy-start(s32[128]{0:T(128)S(1)} %eq.84) | copy-start | bytes 1540
  2.4 27.6 %all-to-all-start = ((s32[8,1,8]{2,1,0:T(1,128)}), s32[8,1,8]{2,1,0:T(1,128)S(1)}, u32[]{:S(2)}, u32[]{:S(2)}) async-start(s32[8,1,8]{2,1,0:T(1,128)} %bitcast.3), calls=%async_computation | async-start | bytes 8192 | tf_op jit(solution)/shard_map/all_to_all | solution.py:47
  10.0 37.2 %copy-start.11 = (f32[8]{0:T(128)S(1)}, f32[8]{0:T(128)}, u32[]{:S(2)}) copy-start(f32[8]{0:T(128)} %param.10) | copy-start | bytes 100
  28.2 65.4 %copy-start.5 = (s32[64]{0:T(128)}, s32[64]{0:T(128)S(1)}, u32[]{:S(2)}) copy-start(s32[64]{0:T(128)S(1)} %eq.95) | copy-start | bytes 772
  28.6 72.2 %copy-start.7 = (s32[1024]{0:T(1024)}, s32[1024]{0:T(1024)S(1)}, u32[]{:S(2)}) copy-start(s32[1024]{0:T(1024)S(1)} %pad_clamp_fusion) | copy-start | bytes 12292
  30.0 13.4 %all-to-all-start.2 = ((f32[8,2,16,128]{3,2,1,0:T(8,128)}), f32[8,2,16,128]{3,2,1,0:T(8,128)S(1)}, u32[]{:S(2)}, u32[]{:S(2)}) async-start(f32[8,2,16,128]{3,2,1,0:T(8,128)} %copy.169), calls=%async_computation.2 | async-start | bytes 262144 | tf_op jit(solution)/shard_map/all_to_all | solution.py:86
  43.3 11.2 %all-to-all-start.1 = ((f32[8,2,16,128]{3,2,1,0:T(8,128)}), f32[8,2,16,128]{3,2,1,0:T(8,128)S(1)}, u32[]{:S(2)}, u32[]{:S(2)}) async-start(f32[8,2,16,128]{3,2,1,0:T(8,128)} %broadcast_select_fusion.4), calls=%async_computation.1 | async-start | bytes 262144 | tf_op jit(solution)/shard_map/all_to_all | solution.py:66
  48.0 101.1 %copy-start.4 = (s32[16]{0:T(128)}, s32[16]{0:T(128)S(1)}, u32[]{:S(2)}) copy-start(s32[16]{0:T(128)S(1)} %select_n.117) | copy-start | bytes 196
  78.0 10.7 %all-to-all-start.4 = ((f32[8,2,16,128]{3,2,1,0:T(8,128)}), f32[8,2,16,128]{3,2,1,0:T(8,128)S(1)}, u32[]{:S(2)}, u32[]{:S(2)}) async-start(f32[8,2,16,128]{3,2,1,0:T(8,128)} %copy.175), calls=%async_computation.4 | async-start | bytes 262144 | tf_op jit(solution)/shard_map/all_to_all | solution.py:86
  88.6 12.2 %all-to-all-start.3 = ((f32[8,2,16,128]{3,2,1,0:T(8,128)}), f32[8,2,16,128]{3,2,1,0:T(8,128)S(1)}, u32[]{:S(2)}, u32[]{:S(2)}) async-start(f32[8,2,16,128]{3,2,1,0:T(8,128)} %broadcast_select_fusion.3), calls=%async_computation.3 | async-start | bytes 262144 | tf_op jit(solution)/shard_map/all_to_all | solution.py:66
  111.7 50.0 %copy-start.3 = (s32[128]{0:T(128)S(1)}, s32[128]{0:T(128)}, u32[]{:S(2)}) copy-start(s32[128]{0:T(128)} %copy-done.2) | copy-start | bytes 1540
  130.5 0.5 copy-start.9
  149.0 17.4 %copy-start.10 = (f32[16]{0:T(128)}, f32[16]{0:T(128)S(1)}, u32[]{:S(2)}) copy-start(f32[16]{0:T(128)S(1)} %psum.37) | copy-start | bytes 196
  149.0 0.6 copy-start.8
  163.0 10.7 %all-to-all-start.6 = ((f32[8,2,16,128]{3,2,1,0:T(8,128)}), f32[8,2,16,128]{3,2,1,0:T(8,128)S(1)}, u32[]{:S(2)}, u32[]{:S(2)}) async-start(f32[8,2,16,128]{3,2,1,0:T(8,128)} %copy.181), calls=%async_computation.6 | async-start | bytes 262144 | tf_op jit(solution)/shard_map/all_to_all | solution.py:86
  173.7 12.2 %all-to-all-start.5 = ((f32[8,2,16,128]{3,2,1,0:T(8,128)}), f32[8,2,16,128]{3,2,1,0:T(8,128)S(1)}, u32[]{:S(2)}, u32[]{:S(2)}) async-start(f32[8,2,16,128]{3,2,1,0:T(8,128)} %broadcast_select_fusion.2), calls=%async_computation.5 | async-start | bytes 262144 | tf_op jit(solution)/shard_map/all_to_all | solution.py:66
  210.2 10.7 %all-to-all-start.8 = ((f32[8,2,16,128]{3,2,1,0:T(8,128)}), f32[8,2,16,128]{3,2,1,0:T(8,128)S(1)}, u32[]{:S(2)}, u32[]{:S(2)}) async-start(f32[8,2,16,128]{3,2,1,0:T(8,128)} %copy.187), calls=%async_computation.8 | async-start | bytes 262144 | tf_op jit(solution)/shard_map/all_to_all | solution.py:86
  220.8 12.3 %all-to-all-start.7 = ((f32[8,2,16,128]{3,2,1,0:T(8,128)}), f32[8,2,16,128]{3,2,1,0:T(8,128)S(1)}, u32[]{:S(2)}, u32[]{:S(2)}) async-start(f32[8,2,16,128]{3,2,1,0:T(8,128)} %broadcast_select_fusion.1), calls=%async_computation.7 | async-start | bytes 262144 | tf_op jit(solution)/shard_map/all_to_all | solution.py:66
  265.9 38.2 %copy-start.1 = (f32[8,16,128]{2,1,0:T(8,128)}, f32[8,16,128]{2,1,0:T(8,128)S(1)}, u32[]{:S(2)}) copy-start(f32[8,16,128]{2,1,0:T(8,128)S(1)} %multiply_reduce_fusion) | copy-start | bytes 196612
  286.4 11.4 %all-to-all-start.10 = ((f32[8,2,16,128]{3,2,1,0:T(8,128)}), f32[8,2,16,128]{3,2,1,0:T(8,128)S(1)}, u32[]{:S(2)}, u32[]{:S(2)}) async-start(f32[8,2,16,128]{3,2,1,0:T(8,128)} %copy.193), calls=%async_computation.10 | async-start | bytes 262144 | tf_op jit(solution)/shard_map/all_to_all | solution.py:86
  297.8 13.7 %all-to-all-start.9 = ((f32[8,2,16,128]{3,2,1,0:T(8,128)}), f32[8,2,16,128]{3,2,1,0:T(8,128)S(1)}, u32[]{:S(2)}, u32[]{:S(2)}) async-start(f32[8,2,16,128]{3,2,1,0:T(8,128)} %broadcast_select_fusion), calls=%async_computation.9 | async-start | bytes 262144 | tf_op jit(solution)/shard_map/all_to_all | solution.py:66
where the time goes:
time: 364 us; the launch traced here: 357 us
  matrix products  138 us (38%)
  blocking collectives  94.4 us (26%)
  starting transfers between devices  51.9 us (14%)
  waiting for transfers between devices  38.8 us (11%)
  local copies, waits for them, and re-layouts  20.8 us (6%)
  other arithmetic  11.5 us (3%)
    dot_general x5, matrix products, apply_h(): jnp.einsum('ikab,ikvb->iva', far_blocks, far_vec, precision=exact_mode)  48.2 us
    psum x2, blocking collectives, squares(): return lax.psum(column_dot(vector, vector), 'rows')  36.3 us
    psum x1, blocking collectives, shards(): summed = lax.psum(partial_gram, 'rows')  34.1 us
    dot_general x5, matrix products, apply_h(): jnp.einsum('ikab,iva->ikvb', far_blocks, vector, precision=exact_mode)  31.9 us
    all_to_all x5, waiting for transfers between devices, apply_h(): lax.all_to_all(outgoing, 'rows', split_axis=0, concat_axis=0, tiled=True)  29.9 us
    dot_general x5, matrix products, apply_h(): jnp.einsum('ikab,ikvb->iva', near_blocks, near_vec, precision=exact_mode)  26.5 us
    all_to_all x5, starting transfers between devices, apply_h(): lax.all_to_all(outgoing, 'rows', split_axis=0, concat_axis=0, tiled=True)  25.1 us
    all_to_all x5, starting transfers between devices, apply_h(): lax.all_to_all(slot_sums, 'rows', split_axis=0, concat_axis=0, tiled=True)  19.5 us
  transfers between devices with their start and end apart: 11, of which 9 were waited for; matrix products, arithmetic and copies ran while one was open for 15% of the time, Pallas kernels for 0%

commit v1 on v0

v1 whole, which is shorter than its diff:
```python
import jax
import jax.numpy as jnp
from jax import lax
from jax.sharding import PartitionSpec as P

CAP = 2


exact_mode = lax.Precision.HIGHEST


def column_dot(first_arr, second_arr):
    return jnp.sum(first_arr * second_arr, axis=(0, 2))


def ordered_lists(need_mask, slot_width):
    ranks = jnp.cumsum(need_mask, axis=1)
    positions = lax.broadcasted_iota(jnp.int32, need_mask.shape, 1)
    columns_out = []
    for slot in range(slot_width):
        hit = (need_mask > 0) & (ranks == slot + 1)
        columns_out.append(jnp.sum(jnp.where(hit, positions, 0), axis=1))
    lists = jnp.stack(columns_out, axis=1)
    live = jnp.sum(need_mask, axis=1, keepdims=True) > 0
    return jnp.where(live, lists, -1)


def filter_factors(alpha_one, beta_one, alpha_two, delta_shift, weights):
    zeta_one = 1.0 / (1.0 + delta_shift * alpha_one)
    zeta_two = (
        zeta_one
        * alpha_one
        / (alpha_two * beta_one * (1.0 - zeta_one) + alpha_one * (1.0 + delta_shift * alpha_two))
    )
    from_start = jnp.sum(
        weights * (alpha_one * zeta_one + alpha_two * beta_one * zeta_one * zeta_two), axis=0
    )
    from_residual = jnp.sum(weights * (alpha_two * zeta_two), axis=0)
    return from_start, from_residual


def shards(hblocks, col_index, right_side, center, shifts, filter_weights):
    block_rows = hblocks.shape[0]
    block_width = hblocks.shape[2]
    local_vecs = right_side.shape[1]
    pole_count = shifts.shape[0]
    peer_count = lax.axis_size("rows")
    slot_width = CAP
    device_index = lax.axis_index("rows")
    own_cols = col_index[:, :block_rows] - device_index * block_rows
    far_cols = col_index[:, block_rows:].reshape(-1)
    near_blocks = hblocks[:, :block_rows]
    far_blocks = hblocks[:, block_rows:]
    every_key = jnp.arange(peer_count * block_rows, dtype=jnp.int32)
    need_mask = (
        jnp.any(far_cols[:, None] == every_key[None, :], axis=0)
        .astype(jnp.int32)
        .reshape(peer_count, block_rows)
    )
    incoming_mask = lax.all_to_all(need_mask, "rows", split_axis=0, concat_axis=0, tiled=True)
    send_lists = ordered_lists(incoming_mask, slot_width)
    my_lists = ordered_lists(need_mask, slot_width)
    owners = lax.broadcasted_iota(jnp.int32, my_lists.shape, 0)
    slot_keys = jnp.where(my_lists >= 0, owners * block_rows + my_lists, -1).reshape(-1)
    slot_total = slot_keys.shape[0]
    matches = far_cols[:, None] == slot_keys[None, :]
    picker = matches.astype(jnp.float32)
    slot_numbers = lax.broadcasted_iota(jnp.int32, matches.shape, 1)
    slot_of_ref = jnp.sum(jnp.where(matches, slot_numbers, 0), axis=1)
    row_numbers = jnp.arange(block_rows, dtype=jnp.int32)[:, None]
    spread = (send_lists.reshape(-1)[None, :] == row_numbers).astype(jnp.float32)
    own_spread = (own_cols.reshape(-1)[None, :] == row_numbers).astype(jnp.float32)
    send_index = jnp.maximum(send_lists, 0)
    send_live = (send_lists >= 0)[:, :, None, None]

    def apply_h(vector):
        far_terms = jnp.einsum("ikab,iva->ikvb", far_blocks, vector, precision=exact_mode).reshape(
            far_cols.shape[0], -1
        )
        slot_sums = jnp.dot(picker.T, far_terms, precision=exact_mode).reshape(
            peer_count, slot_width, local_vecs, block_width
        )
        picked = vector[send_index]
        outgoing = jnp.where(send_live, picked, jnp.zeros_like(picked))
        both = lax.all_to_all(
            jnp.concatenate([outgoing, slot_sums], axis=1),
            "rows",
            split_axis=0,
            concat_axis=0,
            tiled=True,
        )
        arrived = both[:, :slot_width].reshape(slot_total, local_vecs, block_width)
        returned = both[:, slot_width:].reshape(slot_total, -1)
        near_vec = vector[own_cols]
        result = jnp.einsum("ikab,ikvb->iva", near_blocks, near_vec, precision=exact_mode)
        near_terms = jnp.einsum(
            "ikab,iva->ikvb", near_blocks, vector, precision=exact_mode
        ).reshape(block_rows * block_rows, -1)
        result = result + jnp.dot(own_spread, near_terms, precision=exact_mode).reshape(
            vector.shape
        )
        far_vec = arrived[slot_of_ref]
        far_vec = far_vec.reshape(block_rows, -1, local_vecs, block_width)
        result = result + jnp.einsum("ikab,ikvb->iva", far_blocks, far_vec, precision=exact_mode)
        return result + jnp.dot(spread, returned, precision=exact_mode).reshape(vector.shape)

    def wide(per_column):
        return per_column[None, :, None]

    center_value = center[0]
    base_shift = jnp.min(shifts)
    delta_shift = (shifts - base_shift)[:, None]
    start = right_side
    start_image = apply_h(start)
    half_one = start_image - center_value * start
    start_norm, half_norm = lax.psum(
        jnp.stack([column_dot(start, start), column_dot(half_one, half_one)]), "rows"
    )
    alpha_one = start_norm / (half_norm + base_shift * start_norm)
    op_image = apply_h(half_one) - center_value * half_one + base_shift * start
    residual = start - wide(alpha_one) * op_image
    residual_image = apply_h(residual)
    res_norm = lax.psum(column_dot(residual, residual), "rows")
    beta_one = res_norm / start_norm
    direction = residual + wide(beta_one) * start
    half_two = residual_image - center_value * residual + wide(beta_one) * half_one
    energy = lax.psum(
        column_dot(half_two, half_two) + base_shift * column_dot(direction, direction), "rows"
    )
    from_start, from_residual = filter_factors(
        alpha_one, beta_one, res_norm / energy, delta_shift, filter_weights[:, None]
    )
    filtered = wide(from_start) * start + wide(from_residual) * residual
    applied = wide(from_start) * start_image + wide(from_residual) * residual_image
    column_piece = lax.all_gather(filtered, "cols", axis=1, tiled=True)
    correlation = jnp.einsum("iae,ibe->ab", column_piece, filtered, precision=exact_mode)
    projected = jnp.einsum("iae,ibe->ab", column_piece, applied, precision=exact_mode)
    partial_gram = jnp.stack([correlation, projected])
    summed = lax.psum(partial_gram, "rows")
    row_total = peer_count * block_rows * block_width
    return (filtered, summed[0] / row_total, summed[1] / row_total)


def solution(mesh):
    placed = (P("rows", None, None, None), P("rows", None), P("rows", "cols", None), P(), P(), P())
    return jax.shard_map(
        shards,
        mesh=mesh,
        in_specs=placed,
        out_specs=(P("rows", "cols", None), P(None, "cols"), P(None, "cols")),
        check_vma=False,
    )
```

time: 364 us -> 223 us (0.61); the launches traced: 357 us -> 223 us
  matrix products: 138 us -> 79.9 us
  waiting for transfers between devices: 38.8 us -> 4.58 us
  starting transfers between devices: 51.9 us -> 20.4 us
  local copies, waits for them, and re-layouts: 20.8 us -> 12.5 us
  other arithmetic: 11.5 us -> 5.65 us
    all_to_all x10 -> x3, waiting for transfers between devices: 38.8 us -> 4.58 us  [apply_h(): lax.all_to_all(jnp.concatenate([outgoing, slot_sums], axis=1), 'rows', sp...]
    all_to_all x10 -> x3, starting transfers between devices: 44.6 us -> 13.1 us  [apply_h(): lax.all_to_all(jnp.concatenate([outgoing, slot_sums], axis=1), 'rows', sp...]
    dot_general x5 -> x3, matrix products: 48.2 us -> 29 us  [apply_h(): jnp.einsum('ikab,ikvb->iva', far_blocks, far_vec, precision=exact_mode)]
    dot_general x5 -> x3, matrix products: 31.9 us -> 19.2 us  [apply_h(): jnp.einsum('ikab,iva->ikvb', far_blocks, vector, precision=exact_mode)]
    dot_general x5 -> x3, matrix products: 26.5 us -> 15.9 us  [apply_h(): jnp.einsum('ikab,ikvb->iva', near_blocks, near_vec, precision=exact_mode)]
    dot_general x5 -> x3, matrix products: 19.2 us -> 11.5 us  [apply_h(): jnp.einsum('ikab,iva->ikvb', near_blocks, vector, precision=exact_mode)]
    psum x3, blocking collectives: 54.5 us -> 59.2 us  [the longest x1 22.1 us: shards(): lax.psum(jnp.stack([column_dot(start, start), column_dot(half_one, half_o...]
    select_n x5 -> x3, other arithmetic: 4.59 us -> 0.26 us  [apply_h(): outgoing = jnp.where(send_live, picked, jnp.zeros_like(picked))]
  transfers between devices with their start and end apart: 11 -> 4, of which waited for: 9 -> 2; matrix products, arithmetic and copies ran while one was open for 15% -> 15% of each run, Pallas kernels for 0% -> 0%
where the time goes in v1:
time: 223 us
  blocking collectives  98 us (44%)
  matrix products  79.9 us (36%)
  starting transfers between devices  20.4 us (9%)
  local copies, waits for them, and re-layouts  12.5 us (6%)
  other arithmetic  5.65 us (3%)
  waiting for transfers between devices  4.58 us (2%)
    psum x1, blocking collectives, shards(): summed = lax.psum(partial_gram, 'rows')  33 us
    dot_general x3, matrix products, apply_h(): jnp.einsum('ikab,ikvb->iva', far_blocks, far_vec, precision=exact_mode)  29 us
    psum x1, blocking collectives, shards(): lax.psum(jnp.stack([column_dot(start, start), column_dot(half_one, half_o...  22.1 us
    psum x1, blocking collectives, shards(): lax.psum(column_dot(half_two, half_two) + base_shift * column_dot(directi...  20 us
    dot_general x3, matrix products, apply_h(): jnp.einsum('ikab,iva->ikvb', far_blocks, vector, precision=exact_mode)  19.2 us
    psum x1, blocking collectives, shards(): res_norm = lax.psum(column_dot(residual, residual), 'rows')  17.1 us
    dot_general x3, matrix products, apply_h(): jnp.einsum('ikab,ikvb->iva', near_blocks, near_vec, precision=exact_mode)  15.9 us
    all_to_all x3, starting transfers between devices, apply_h(): lax.all_to_all(jnp.concatenate([outgoing, slot_sums], axis=1), 'rows', sp...  13.1 us
  transfers between devices with their start and end apart: 4, of which 2 were waited for; matrix products, arithmetic and copies ran while one was open for 15% of the time, Pallas kernels for 0%

profile of v1, /device:TPU:0, one launch (start us, length us, event | category | flops | bytes accessed | tf_op | source)
XLA Modules:
  0.0 222.7 jit_solution(15622802453715695048)
XLA Ops:
  0.7 0.8 slice.38
  1.7 0.7 reshape.294
  2.4 7.3 %all-to-all-start = ((s32[8,1,8]{2,1,0:T(1,128)}), s32[8,1,8]{2,1,0:T(1,128)S(1)}, u32[]{:S(2)}, u32[]{:S(2)}) async-start(s32[8,1,8]{2,1,0:T(1,128)} %bitcast.9), calls=%async_computation | async-start | bytes 8192 | tf_op jit(solution)/shard_map/all_to_all | solution.py:60
  9.7 0.2 reduce_window_sum.18
  10.0 6.4 %fusion.10 = f32[8,16,16,128]{3,1,2,0:T(8,128)S(1)} fusion(f32[8,24,128,128]{3,2,1,0:T(8,128)} %param.6, f32[8,16,128]{2,1,0:T(8,128)} %param.8), kind=kOutput, calls=%fused_computation.19 | convolution fusion | flops 402653184 | bytes 9502720 | tf_op jit(solution)/shard_map/ikab,iva->ikvb/dot_general | solution.py:77
  16.4 3.9 %fusion.24 = f32[8,8,16,128]{3,2,1,0:T(8,128)S(1)} fusion(f32[8,24,128,128]{3,2,1,0:T(8,128)} %param.6, f32[8,16,128]{2,1,0:T(8,128)} %param.8), kind=kOutput, calls=%fused_computation.33 | convolution fusion | flops 201326592 | bytes 4784128 | tf_op jit(solution)/shard_map/ikab,iva->ikvb/dot_general | solution.py:96
  20.3 0.3 copy.208
  20.7 0.3 copy.107
  21.0 0.2 select_reduce_fusion.2
  21.3 0.6 fusion.126
  22.2 0.6 reduce_min.9
  22.8 0.6 broadcast_subtract_fusion
  23.5 0.4 fusion.96
  24.6 0.6 gather_fusion
  25.2 0.2 reduce_window_sum.17
  25.5 0.2 reduce_sum.129
  26.0 0.6 gather_fusion.1
  26.7 0.7 copy.108
  27.4 6.0 %all-to-all-start.1 = ((f32[8,4,16,128]{3,2,1,0:T(8,128)}), f32[8,4,16,128]{3,2,1,0:T(8,128)S(1)}, u32[]{:S(2)}, u32[]{:S(2)}) async-start(f32[8,4,16,128]{3,2,1,0:T(8,128)} %copy.108), calls=%async_computation.1 | async-start | bytes 524288 | tf_op jit(solution)/shard_map/all_to_all | solution.py:85
  33.4 5.3 %fusion.87 = f32[8,16,128]{2,1,0:T(8,128)S(1)} fusion(f32[8,8,16,128]{3,2,1,0:T(8,128)S(1)} %bitcast.295, f32[8,24,128,128]{3,2,1,0:T(8,128)} %param.6, f32[8,16,128]{2,0,1:T(8,128)S(1)} %fusion.96), kind=kOutput, calls=%fused_computation.54 | convolution fusion | flops 201342976 | bytes 4849664 | tf_op jit(solution)/shard_map/ikab,ikvb->iva/dot_general | solution.py:95
  38.9 3.0 %all-to-all-done.1 = f32[8,4,16,128]{3,2,1,0:T(8,128)S(1)} async-done(((f32[8,4,16,128]{3,2,1,0:T(8,128)}), f32[8,4,16,128]{3,2,1,0:T(8,128)S(1)}, u32[]{:S(2)}, u32[]{:S(2)}) %all-to-all-start.1) | async-done | bytes 262176 | tf_op jit(solution)/shard_map/all_to_all | solution.py:85
  42.0 0.2 fusion.105
  42.2 0.8 gather_fusion.2
  42.9 9.5 %multiply_reduce_fusion.3 = (f32[16]{0:T(128)S(1)}, f32[8,16,128]{2,1,0:T(8,128)S(1)}, f32[16]{0:T(128)S(1)}, f32[8,16,128]{2,1,0:T(8,128)S(1)}) fusion(f32[8,16,128]{2,1,0:T(8,128)S(1)} %copy-done, f32[]{:T(128)} %bitcast.277, f32[8,16,128]{2,0,1:T(8,128)S(1)} %fusion.105, f32[8,16,128]{2,1,0:T(8,128)S(1)} %fusion.87, ...), kind=kOutput, calls=%fused_computation.103 | convolution fusion | flops 402784224 | bytes 9765504 | tf_op jit(solution)/shard_map/ikab,ikvb->iva/dot_general | solution.py:104
  52.4 6.4 %fusion.6 = f32[8,16,16,128]{3,1,2,0:T(8,128)S(1)} fusion(f32[8,24,128,128]{3,2,1,0:T(8,128)} %param.6, f32[8,16,128]{2,1,0:T(8,128)S(1)} %get-tuple-element.14), kind=kOutput, calls=%fused_computation.15 | convolution fusion | flops 402653184 | bytes 9502720 | tf_op jit(solution)/shard_map/ikab,iva->ikvb/dot_general | solution.py:77
  58.8 0.6 gather_fusion.4
  59.4 3.8 %fusion.27 = f32[8,8,16,128]{3,2,1,0:T(8,128)S(1)} fusion(f32[8,24,128,128]{3,2,1,0:T(8,128)} %param.6, f32[8,16,128]{2,1,0:T(8,128)S(1)} %get-tuple-element.14), kind=kOutput, calls=%fused_computation.34 | convolution fusion | flops 201326592 | bytes 4784128 | tf_op jit(solution)/shard_map/ikab,iva->ikvb/dot_general | solution.py:96
  63.2 0.3 copy.207
  63.5 0.3 copy.116
  63.9 0.6 fusion.124
  64.6 0.7 copy.117
  65.3 3.4 %all-to-all-start.2 = ((f32[8,4,16,128]{3,2,1,0:T(8,128)}), f32[8,4,16,128]{3,2,1,0:T(8,128)S(1)}, u32[]{:S(2)}, u32[]{:S(2)}) async-start(f32[8,4,16,128]{3,2,1,0:T(8,128)} %copy.117), calls=%async_computation.2 | async-start | bytes 524288 | tf_op jit(solution)/shard_map/all_to_all | solution.py:85
  68.8 0.4 fusion.93
  69.2 22.1 %psum.28 = f32[2,16]{1,0:T(2,128)S(1)} all-reduce(f32[2,16]{1,0:T(2,128)S(1)} %pad_maximum_fusion.4), channel_id=1, replica_groups=mesh['rows'=8,'cols'=4] {'rows'}, use_global_device_ids=true, to_apply=%region_12.13 | all-reduce | flops 32 | bytes 256 | tf_op jit(solution)/shard_map/psum | solution.py:116
  91.3 0.7 fusion.153
  91.9 0.6 gather_fusion.3
  92.6 5.3 %fusion.84 = f32[8,16,128]{2,1,0:T(8,128)S(1)} fusion(f32[8,8,16,128]{3,2,1,0:T(8,128)S(1)} %bitcast.297, f32[8,24,128,128]{3,2,1,0:T(8,128)} %param.6, f32[8,16,128]{2,0,1:T(8,128)S(1)} %fusion.93), kind=kOutput, calls=%fused_computation.53 | convolution fusion | flops 201342976 | bytes 4849664 | tf_op jit(solution)/shard_map/ikab,ikvb->iva/dot_general | solution.py:95
  97.9 0.2 fusion.102
  98.1 0.8 gather_fusion.5
  98.9 10.1 %multiply_reduce_fusion.2 = (f32[16]{0:T(128)S(1)}, f32[8,16,128]{2,1,0:T(8,128)S(1)}) fusion(f32[8,16,128]{2,1,0:T(8,128)S(1)} %copy-done, f32[]{:T(128)} %reduce_min.9, f32[8,16,128]{2,1,0:T(8,128)S(1)} %get-tuple-element.14, f32[]{:T(128)} %bitcast.279, f32[8,16,128]{2,0,1:T(8,128)S(1)} %fusion.102, f32[8,16,128]{2,1,0:T(8,128)S(1)} %fusion.84, ...), kind=kOutput, calls=%fused_computation.102 | convolution fusion | flops 402817024 | bytes 9766016 | tf_op jit(solution)/shard_map/ikab,ikvb->iva/dot_general | solution.py:104
  109.0 6.4 %fusion.2 = f32[8,16,16,128]{3,1,2,0:T(8,128)S(1)} fusion(f32[8,24,128,128]{3,2,1,0:T(8,128)} %param.6, f32[8,16,128]{2,1,0:T(8,128)S(1)} %get-tuple-element.30), kind=kOutput, calls=%fused_computation.11 | convolution fusion | flops 402653184 | bytes 9502720 | tf_op jit(solution)/shard_map/ikab,iva->ikvb/dot_general | solution.py:77
  115.4 0.6 gather_fusion.7
  115.9 3.8 %fusion.30 = f32[8,8,16,128]{3,2,1,0:T(8,128)S(1)} fusion(f32[8,24,128,128]{3,2,1,0:T(8,128)} %param.6, f32[8,16,128]{2,1,0:T(8,128)S(1)} %get-tuple-element.30), kind=kOutput, calls=%fused_computation.35 | convolution fusion | flops 201326592 | bytes 4784128 | tf_op jit(solution)/shard_map/ikab,iva->ikvb/dot_general | solution.py:96
  119.8 17.1 %psum.29 = f32[16]{0:T(128)S(1)} all-reduce(f32[16]{0:T(128)S(1)} %get-tuple-element.29), channel_id=1, replica_groups=mesh['rows'=8,'cols'=4] {'rows'}, use_global_device_ids=true, to_apply=%region_15.16 | all-reduce | flops 16 | bytes 128 | tf_op jit(solution)/shard_map/psum | solution.py:123
  136.9 0.3 copy.206
  137.2 0.3 copy.123
  137.6 0.6 fusion.122
  138.3 0.7 copy.124
  139.0 3.7 %all-to-all-start.3 = ((f32[8,4,16,128]{3,2,1,0:T(8,128)}), f32[8,4,16,128]{3,2,1,0:T(8,128)S(1)}, u32[]{:S(2)}, u32[]{:S(2)}) async-start(f32[8,4,16,128]{3,2,1,0:T(8,128)} %copy.124), calls=%async_computation.3 | async-start | bytes 524288 | tf_op jit(solution)/shard_map/all_to_all | solution.py:85
  142.7 0.4 fusion.90
  143.1 0.6 gather_fusion.6
  143.8 5.3 %fusion.81 = f32[8,16,128]{2,1,0:T(8,128)S(1)} fusion(f32[8,8,16,128]{3,2,1,0:T(8,128)S(1)} %bitcast.296, f32[8,24,128,128]{3,2,1,0:T(8,128)} %param.6, f32[8,16,128]{2,0,1:T(8,128)S(1)} %fusion.90), kind=kOutput, calls=%fused_computation.52 | convolution fusion | flops 201342976 | bytes 4849664 | tf_op jit(solution)/shard_map/ikab,ikvb->iva/dot_general | solution.py:95
  149.1 1.5 all-to-all-done.3
  150.6 0.2 fusion.99
  150.8 0.8 gather_fusion.8
  151.6 9.5 %multiply_reduce_fusion = (f32[16]{0:T(128)S(1)}, f32[16]{0:T(128)S(1)}, f32[8,16,128]{2,1,0:T(8,128)S(1)}) fusion(f32[8,16,128]{2,1,0:T(8,128)S(1)} %get-tuple-element.30, f32[8,16,128]{2,1,0:T(8,128)S(1)} %copy-done, f32[16]{0:T(128)S(1)} %bitcast_divide_fusion, f32[8,16,128]{2,1,0:T(8,128)S(1)} %get-tuple-element.14, f32[]{:T(128)} %bitcast.278, ...), kind=kOutput, calls=%fused_computation.100 | convolution fusion | flops 402849760 | bytes 9831104 | tf_op jit(solution)/shard_map/ikab,ikvb->iva/dot_general | solution.py:104
  161.1 0.7 multiply_add_fusion.1
  161.7 0.7 fusion.154
  162.4 20.0 %psum.30 = f32[16]{0:T(128)S(1)} all-reduce(f32[16]{0:T(128)S(1)} %multiply_add_fusion.1), channel_id=1, replica_groups=mesh['rows'=8,'cols'=4] {'rows'}, use_global_device_ids=true, to_apply=%region_18.19 | all-reduce | flops 16 | bytes 128 | tf_op jit(solution)/shard_map/psum | solution.py:127
  182.6 5.8 %all_gather.3 = f32[8,64,128]{2,1,0:T(8,128)S(1)} all-gather(f32[8,16,128]{2,1,0:T(8,128)S(1)} %multiply_add_fusion), channel_id=1, replica_groups=mesh['rows'=8,'cols'=4] {'cols'}, dimensions={1}, use_global_device_ids=true | all-gather | bytes 327680 | tf_op jit(solution)/shard_map/all_gather | solution.py:135
  188.4 0.3 convolution_bitcast_fusion.1
  188.7 0.4 convolution_bitcast_fusion
  189.1 33.0 %psum.31 = f32[2,64,16]{1,2,0:T(8,128)S(1)} all-reduce(f32[2,64,16]{1,2,0:T(8,128)S(1)} %pad_maximum_fusion.3), channel_id=1, replica_groups=mesh['rows'=8,'cols'=4] {'rows'}, use_global_device_ids=true, to_apply=%region_21.22 | all-reduce | flops 2048 | bytes 16384 | tf_op jit(solution)/shard_map/psum | solution.py:139
  222.1 0.6 fusion.120
  (53 shorter events, 2.0 us)
Async XLA Ops:
  0.6 21.2 %copy-start.2 = (s32[8,24]{1,0:T(8,128)S(1)}, s32[8,24]{1,0:T(8,128)}, u32[]{:S(2)}) copy-start(s32[8,24]{1,0:T(8,128)} %param.7) | copy-start | bytes 2308
  0.6 23.9 %copy-start = (f32[8,16,128]{2,1,0:T(8,128)S(1)}, f32[8,16,128]{2,1,0:T(8,128)}, u32[]{:S(2)}) copy-start(f32[8,16,128]{2,1,0:T(8,128)} %param.8) | copy-start | bytes 196612
  0.7 21.6 %copy-start.4 = (f32[8]{0:T(128)S(1)}, f32[8]{0:T(128)}, u32[]{:S(2)}) copy-start(f32[8]{0:T(128)} %param.10) | copy-start | bytes 100
  2.4 22.9 %all-to-all-start = ((s32[8,1,8]{2,1,0:T(1,128)}), s32[8,1,8]{2,1,0:T(1,128)S(1)}, u32[]{:S(2)}, u32[]{:S(2)}) async-start(s32[8,1,8]{2,1,0:T(1,128)} %bitcast.9), calls=%async_computation | async-start | bytes 8192 | tf_op jit(solution)/shard_map/all_to_all | solution.py:60
  27.4 14.5 %all-to-all-start.1 = ((f32[8,4,16,128]{3,2,1,0:T(8,128)}), f32[8,4,16,128]{3,2,1,0:T(8,128)S(1)}, u32[]{:S(2)}, u32[]{:S(2)}) async-start(f32[8,4,16,128]{3,2,1,0:T(8,128)} %copy.108), calls=%async_computation.1 | async-start | bytes 524288 | tf_op jit(solution)/shard_map/all_to_all | solution.py:85
  65.3 32.5 %all-to-all-start.2 = ((f32[8,4,16,128]{3,2,1,0:T(8,128)}), f32[8,4,16,128]{3,2,1,0:T(8,128)S(1)}, u32[]{:S(2)}, u32[]{:S(2)}) async-start(f32[8,4,16,128]{3,2,1,0:T(8,128)} %copy.117), calls=%async_computation.2 | async-start | bytes 524288 | tf_op jit(solution)/shard_map/all_to_all | solution.py:85
  137.2 45.2 %copy-start.3 = (f32[8]{0:T(128)S(1)}, f32[8]{0:T(128)}, u32[]{:S(2)}) copy-start(f32[8]{0:T(128)} %param.11) | copy-start | bytes 100
  139.0 11.6 %all-to-all-start.3 = ((f32[8,4,16,128]{3,2,1,0:T(8,128)}), f32[8,4,16,128]{3,2,1,0:T(8,128)S(1)}, u32[]{:S(2)}, u32[]{:S(2)}) async-start(f32[8,4,16,128]{3,2,1,0:T(8,128)} %copy.124), calls=%async_computation.3 | async-start | bytes 524288 | tf_op jit(solution)/shard_map/all_to_all | solution.py:85
  182.6 40.1 %copy-start.1 = (f32[8,16,128]{2,1,0:T(8,128)}, f32[8,16,128]{2,1,0:T(8,128)S(1)}, u32[]{:S(2)}) copy-start(f32[8,16,128]{2,1,0:T(8,128)S(1)} %multiply_add_fusion) | copy-start | bytes 196612

commit v2 on v1

--- a/solution.py
+++ b/solution.py
@@ -1,6 +1,10 @@
+import functools
+
 import jax
 import jax.numpy as jnp
 from jax import lax
+from jax.experimental import pallas as pl
+from jax.experimental.pallas import tpu as pltpu
 from jax.sharding import PartitionSpec as P
 
 CAP = 2
@@ -141,10 +145,409 @@
     return (filtered, summed[0] / row_total, summed[1] / row_total)
 
 
+def split(value):
+    high = value.astype(jnp.bfloat16)
+    low = (value - high.astype(jnp.float32)).astype(jnp.bfloat16)
+    return high, low
+
+
+def pack_kernel(index_ref, blocks_ref, high_ref, low_ref, acc):
+    row = pl.program_id(0)
+    width = blocks_ref.shape[-1]
+    acc[...] = jnp.zeros_like(acc)
+    for k in range(blocks_ref.shape[1]):
+        spot = index_ref[row, k]
+        acc[spot] = acc[spot] + blocks_ref[0, k]
+    for spot in range(acc.shape[0]):
+        high, low = split(acc[spot])
+        high_ref[:, spot * width : (spot + 1) * width] = high
+        low_ref[:, spot * width : (spot + 1) * width] = low
+
+
+def pack_blocks(index, hblocks, spots):
+    block_rows, per_row, width, _ = hblocks.shape
+    out = jax.ShapeDtypeStruct((block_rows * width, spots * width), jnp.bfloat16)
+    out_spec = pl.BlockSpec((width, spots * width), lambda i, index_ref: (i, 0))
+    return pl.pallas_call(
+        pack_kernel,
+        grid_spec=pltpu.PrefetchScalarGridSpec(
+            num_scalar_prefetch=1,
+            grid=(block_rows,),
+            in_specs=[
+                pl.BlockSpec((1, per_row, width, width), lambda i, index_ref: (i, 0, 0, 0))
+            ],
+            out_specs=[out_spec, out_spec],
+            scratch_shapes=[pltpu.VMEM((spots, width, width), jnp.float32)],
+        ),
+        out_shape=[out, out],
+        compiler_params=pltpu.CompilerParams(vmem_limit_bytes=16 << 20),
+    )(index, hblocks)
+
+
+def filter_kernel(
+    n_rows,
+    n_cols,
+    center_ref,
+    shifts_ref,
+    weights_ref,
+    vec_ref,
+    lists_ref,
+    high_hbm,
+    low_hbm,
+    out_ref,
+    gram_ref,
+    ritz_ref,
+    high,
+    low,
+    lists,
+    first_send,
+    first_recv,
+    vec_send,
+    vec_recv,
+    prod_send,
+    prod_recv,
+    col_start,
+    col_res,
+    res_send,
+    energy_send,
+    energy_recv,
+    factor_send,
+    factors,
+    gram_send,
+    gram_recv,
+    load_sem,
+    list_sems,
+    vec_sems,
+    prod_sems,
+    col_sems,
+    energy_sems,
+    gram_sems,
+):
+    block_rows, vecs, width = vec_ref.shape
+    mine = block_rows * width
+    pair = CAP * width
+    peers = n_rows - 1
+    me = lax.axis_index("rows")
+    me_col = lax.axis_index("cols")
+    pending = []
+
+    loads = [
+        pltpu.make_async_copy(high_hbm, high, load_sem.at[0]),
+        pltpu.make_async_copy(low_hbm, low, load_sem.at[1]),
+    ]
+    for load in loads:
+        load.start()
+
+    barrier = pltpu.get_barrier_semaphore()
+    for step in range(1, n_rows):
+        pl.semaphore_signal(barrier, inc=1, device_id={"rows": lax.rem(me + step, n_rows)})
+    for step in range(1, n_cols):
+        pl.semaphore_signal(barrier, inc=1, device_id={"cols": lax.rem(me_col + step, n_cols)})
+    pl.semaphore_wait(barrier, peers + n_cols - 1)
+
+    def to_row(src, dst, sems, step):
+        copy = pltpu.make_async_remote_copy(
+            src_ref=src,
+            dst_ref=dst,
+            send_sem=sems.at[0, step - 1],
+            recv_sem=sems.at[1, peers - step],
+            device_id={"rows": lax.rem(me + step, n_rows)},
+            device_id_type=pl.DeviceIdType.MESH,
+        )
+        copy.start()
+        pending.append(copy)
+        return copy
+
+    def to_col(src, dst, sems, step):
+        copy = pltpu.make_async_remote_copy(
+            src_ref=src,
+            dst_ref=dst,
+            send_sem=sems.at[0, step - 1],
+            recv_sem=sems.at[1, n_cols - 1 - step],
+            device_id={"cols": lax.rem(me_col + step, n_cols)},
+            device_id_type=pl.DeviceIdType.MESH,
+        )
+        copy.start()
+        pending.append(copy)
+        return copy
+
+    def arrive(copies):
+        for copy in copies:
+            copy.wait_recv()
+
+    list_copies = [
+        to_row(lists_ref.at[step - 1], lists.at[peers - step], list_sems, step)
+        for step in range(1, n_rows)
+    ]
+
+    def flat(ref):
+        return jnp.concatenate([ref[i] for i in range(block_rows)], axis=1)
+
+    start = flat(vec_ref)
+
+    def named(step, slot, row):
+        mask = lists[step - 1, slot] == row
+        return jnp.concatenate([mask.astype(jnp.float32)] * (vecs // 8), axis=0) > 0.5
+
+    def dot(a, b, transposed):
+        return lax.dot_general(
+            a, b, (((1,), (1 if transposed else 0,)), ((), ())),
+            preferred_element_type=jnp.float32,
+        )
+
+    def times(both, top, columns, transposed):
+        wide_part = dot(both, high[:, columns], transposed)
+        count = top.shape[0]
+        return wide_part[:count] + wide_part[count:] + dot(top, low[:, columns], transposed)
+
+    def apply_h(turn, vector, extra):
+        copies = []
+        for step in range(1, n_rows):
+            parts = []
+            for slot in range(CAP):
+                picked = jnp.zeros((vecs, width), jnp.float32)
+                for row in range(block_rows):
+                    piece = vector[:, row * width : (row + 1) * width]
+                    picked = jnp.where(named(step, slot, row), piece, picked)
+                parts.append(picked)
+            if extra is None:
+                out, into = first_send.at[step - 1], first_recv.at[peers - step]
+            else:
+                parts.append(extra)
+                out, into = vec_send.at[turn - 1, step - 1], vec_recv.at[turn - 1, peers - step]
+            out[...] = jnp.concatenate(parts, axis=1)
+            copies.append(to_row(out, into, vec_sems.at[turn], step))
+        top, bottom = split(vector)
+        both = jnp.concatenate([top, bottom], axis=0)
+        if turn == 0:
+            for load in loads:
+                load.wait()
+        products = []
+        for step in range(1, n_rows):
+            columns = slice(mine + (step - 1) * pair, mine + step * pair)
+            prod_send[turn, step - 1] = times(both, top, columns, False)
+            products.append(
+                to_row(
+                    prod_send.at[turn, step - 1],
+                    prod_recv.at[turn, peers - step],
+                    prod_sems.at[turn],
+                    step,
+                )
+            )
+        near = slice(0, mine)
+        result = times(both, top, near, False) + times(both, top, near, True)
+        arrive(copies)
+        source = first_recv if extra is None else vec_recv.at[turn - 1]
+        far = jnp.concatenate([source[step - 1, :, :pair] for step in range(1, n_rows)], axis=1)
+        total = extra
+        if extra is not None:
+            for step in range(1, n_rows):
+                total = total + source[step - 1, :, pair:]
+        top, bottom = split(far)
+        both = jnp.concatenate([top, bottom], axis=0)
+        result = result + times(both, top, slice(mine, mine + peers * pair), True)
+        arrive(products)
+        pieces = []
+        for row in range(block_rows):
+            piece = result[:, row * width : (row + 1) * width]
+            for step in range(1, n_rows):
+                for slot in range(CAP):
+                    back = prod_recv[turn, step - 1, :, slot * width : (slot + 1) * width]
+                    piece = piece + jnp.where(named(step, slot, row), back, 0.0)
+            pieces.append(piece)
+        return jnp.concatenate(pieces, axis=1), total
+
+    def column_sum(value):
+        return jnp.sum(value, axis=1, keepdims=True)
+
+    center = center_ref[0]
+    poles = [shifts_ref[m] for m in range(shifts_ref.shape[0])]
+    base = functools.reduce(jnp.minimum, poles)
+    lane = lax.broadcasted_iota(jnp.int32, (vecs, width), 1)
+    all_lanes = jnp.zeros((vecs, width), jnp.float32)
+
+    col_copies = [
+        to_col(vec_ref, col_start.at[me_col], col_sems.at[0], step) for step in range(1, n_cols)
+    ]
+    col_start[me_col] = vec_ref[...]
+    arrive(list_copies)
+    start_image, _ = apply_h(0, start, None)
+    half_one = start_image - center * start
+    own_sums = jnp.where(lane == 0, column_sum(start * start), column_sum(half_one * half_one))
+    second, sums = apply_h(1, half_one, own_sums)
+    start_norm = sums[:, 0:1]
+    half_norm = sums[:, 1:2]
+    alpha_one = start_norm / (half_norm + base * start_norm)
+    op_image = second - center * half_one + base * start
+    residual = start - alpha_one * op_image
+    for row in range(block_rows):
+        res_send[row] = residual[:, row * width : (row + 1) * width]
+    col_res[me_col] = res_send[...]
+    col_copies += [
+        to_col(res_send, col_res.at[me_col], col_sems.at[1], step) for step in range(1, n_cols)
+    ]
+    own_norm = column_sum(residual * residual) + all_lanes
+    residual_image, sums = apply_h(2, residual, own_norm)
+    res_norm = sums[:, 0:1]
+    beta = res_norm / start_norm
+    direction = residual + beta * start
+    half_two = residual_image - center * residual + beta * half_one
+    own_energy = column_sum(half_two * half_two + base * (direction * direction)) + all_lanes
+    energy_send[...] = own_energy
+    energy_copies = [
+        to_row(energy_send, energy_recv.at[peers - step], energy_sems, step)
+        for step in range(1, n_rows)
+    ]
+    arrive(energy_copies)
+    energy = own_energy
+    for step in range(1, n_rows):
+        energy = energy + energy_recv[step - 1]
+    alpha_one = alpha_one + all_lanes
+    beta = beta + all_lanes
+    alpha_two = res_norm / energy
+    from_start = all_lanes
+    from_residual = all_lanes
+    for m, pole in enumerate(poles):
+        delta = pole - base
+        zeta_one = 1.0 / (1.0 + delta * alpha_one)
+        zeta_two = (
+            zeta_one
+            * alpha_one
+            / (
+                alpha_two * beta * (1.0 - zeta_one)
+                + alpha_one * (1.0 + delta * alpha_two)
+            )
+        )
+        weight = weights_ref[m]
+        from_start = from_start + weight * (
+            alpha_one * zeta_one + alpha_two * beta * zeta_one * zeta_two
+        )
+        from_residual = from_residual + weight * (alpha_two * zeta_two)
+    factor_send[...] = jnp.where(lane == 0, from_start, from_residual)
+    factors[me_col] = factor_send[...]
+    col_copies += [
+        to_col(factor_send, factors.at[me_col], col_sems.at[2], step)
+        for step in range(1, n_cols)
+    ]
+    along_start, along_res = from_start[:, 0:1], from_residual[:, 0:1]
+    filtered = along_start * start + along_res * residual
+    applied = along_start * start_image + along_res * residual_image
+    for row in range(block_rows):
+        out_ref[row] = filtered[:, row * width : (row + 1) * width]
+    own = jnp.concatenate([filtered, applied], axis=0)
+    arrive(col_copies)
+    every = jnp.concatenate(
+        [
+            factors[c, :, 0:1] * flat(col_start.at[c]) + factors[c, :, 1:2] * flat(col_res.at[c])
+            for c in range(n_cols)
+        ],
+        axis=0,
+    )
+    top, bottom = split(own)
+    every_top, every_bottom = split(every)
+    both = dot(jnp.concatenate([top, bottom], axis=0), every_top, True)
+    count = 2 * vecs
+    partial = both[:count] + both[count:] + dot(top, every_bottom, True)
+    gram_send[...] = jnp.concatenate([partial[:vecs], partial[vecs:]], axis=1)
+    gram_recv[me] = gram_send[...]
+    gram_copies = [
+        to_row(gram_send, gram_recv.at[me], gram_sems, step) for step in range(1, n_rows)
+    ]
+    arrive(gram_copies)
+    summed = gram_recv[0]
+    for device in range(1, n_rows):
+        summed = summed + gram_recv[device]
+    turned = jnp.transpose(summed * (1.0 / (n_rows * mine)))
+    columns = n_cols * vecs
+    gram_ref[...] = turned[:columns]
+    ritz_ref[...] = turned[columns:]
+    for copy in pending:
+        copy.wait_send()
+
+
+def fused_shards(
+    n_rows, n_cols, hblocks, col_index, right_side, center, shifts, filter_weights
+):
+    block_rows, _, width, _ = hblocks.shape
+    vecs = right_side.shape[1]
+    peers = n_rows - 1
+    spots = block_rows + CAP * peers
+    mine = block_rows * width
+    me = lax.axis_index("rows")
+    far = col_index[:, block_rows:]
+    owner = far // block_rows
+    row = far - owner * block_rows
+    ahead = lax.rem(owner - me + n_rows, n_rows)
+    hit = ahead[None] == jnp.arange(1, n_rows, dtype=jnp.int32)[:, None, None]
+    low_row = jnp.min(jnp.where(hit, row[None], block_rows), axis=(1, 2))
+    high_row = jnp.max(jnp.where(hit, row[None], -1), axis=(1, 2))
+    last = jnp.sum(jnp.where(hit, high_row[:, None, None], 0), axis=0)
+    slot = block_rows + CAP * (ahead - 1) + (row == last).astype(jnp.int32)
+    index = jnp.concatenate([col_index[:, :block_rows] - me * block_rows, slot], axis=1)
+    lists = jnp.broadcast_to(
+        jnp.stack([low_row, high_row], axis=1)[:, :, None, None], (peers, CAP, 8, width)
+    )
+    high, low = pack_blocks(index, hblocks, spots)
+    columns = n_cols * vecs
+    pair = CAP * width
+    vmem = pl.BlockSpec(memory_space=pltpu.VMEM)
+    smem = pl.BlockSpec(memory_space=pltpu.SMEM)
+    anywhere = pl.BlockSpec(memory_space=pl.ANY)
+    f32 = jnp.float32
+    return pl.pallas_call(
+        functools.partial(filter_kernel, n_rows, n_cols),
+        out_shape=[
+            jax.ShapeDtypeStruct(right_side.shape, f32),
+            jax.ShapeDtypeStruct((columns, vecs), f32),
+            jax.ShapeDtypeStruct((columns, vecs), f32),
+        ],
+        in_specs=[smem, smem, smem, vmem, vmem, anywhere, anywhere],
+        out_specs=[vmem, vmem, vmem],
+        scratch_shapes=[
+            pltpu.VMEM((mine, spots * width), jnp.bfloat16),
+            pltpu.VMEM((mine, spots * width), jnp.bfloat16),
+            pltpu.VMEM((peers, CAP, 8, width), jnp.int32),
+            pltpu.VMEM((peers, vecs, pair), f32),
+            pltpu.VMEM((peers, vecs, pair), f32),
+            pltpu.VMEM((2, peers, vecs, pair + width), f32),
+            pltpu.VMEM((2, peers, vecs, pair + width), f32),
+            pltpu.VMEM((3, peers, vecs, pair), f32),
+            pltpu.VMEM((3, peers, vecs, pair), f32),
+            pltpu.VMEM((n_cols,) + right_side.shape, f32),
+            pltpu.VMEM((n_cols,) + right_side.shape, f32),
+            pltpu.VMEM(right_side.shape, f32),
+            pltpu.VMEM((vecs, width), f32),
+            pltpu.VMEM((peers, vecs, width), f32),
+            pltpu.VMEM((vecs, width), f32),
+            pltpu.VMEM((n_cols, vecs, width), f32),
+            pltpu.VMEM((vecs, 2 * columns), f32),
+            pltpu.VMEM((n_rows, vecs, 2 * columns), f32),
+            pltpu.SemaphoreType.DMA((2,)),
+            pltpu.SemaphoreType.DMA((2, peers)),
+            pltpu.SemaphoreType.DMA((3, 2, peers)),
+            pltpu.SemaphoreType.DMA((3, 2, peers)),
+            pltpu.SemaphoreType.DMA((3, 2, n_cols - 1)),
+            pltpu.SemaphoreType.DMA((2, peers)),
+            pltpu.SemaphoreType.DMA((2, peers)),
+        ],
+        compiler_params=pltpu.CompilerParams(
+            collective_id=0, has_side_effects=True, vmem_limit_bytes=40 << 20
+        ),
+    )(center, shifts, filter_weights, right_side, lists, high, low)
+
+
 def solution(mesh):
     placed = (P("rows", None, None, None), P("rows", None), P("rows", "cols", None), P(), P(), P())
+    n_rows, n_cols = mesh.shape["rows"], mesh.shape["cols"]
+
+    def body(hblocks, *rest):
+        block_rows, per_row = hblocks.shape[:2]
+        if CAP * (n_rows - 1) * block_rows <= block_rows * per_row:
+            return fused_shards(n_rows, n_cols, hblocks, *rest)
+        return shards(hblocks, *rest)
+
     return jax.shard_map(
-        shards,
+        body,
         mesh=mesh,
         in_specs=placed,
         out_specs=(P("rows", "cols", None), P(None, "cols"), P(None, "cols")),

time: 223 us -> 69.5 us (0.31)
  blocking collectives: 98 us -> 0 us
  matrix products: 79.9 us -> 0 us
  Pallas kernels: 0 us -> 58.3 us
  starting transfers between devices: 20.4 us -> 0 us
  local copies, waits for them, and re-layouts: 12.5 us -> 6.73 us
  waiting for transfers between devices: 4.58 us -> 0 us
  other arithmetic: 5.65 us -> 2.82 us
    psum x4 -> x0, blocking collectives: 92.2 us -> none  [the longest x1 33 us: shards(): summed = lax.psum(partial_gram, 'rows')]
    dot_general x23 -> x0, matrix products: 79.9 us -> none  [the longest x3 29 us: apply_h(): jnp.einsum('ikab,ikvb->iva', far_blocks, far_vec, precision=exact_mode)]
    pallas_call x0 -> x2, Pallas kernels: none -> 58.3 us  [the longest x1 53.7 us: fused_shards(): pl.pallas_call(functools.partial(filter_kernel, n_rows, n_cols), out_shap...]
    all_to_all x4 -> x0, starting transfers between devices: 20.4 us -> none  [the longest x3 13.1 us: apply_h(): lax.all_to_all(jnp.concatenate([outgoing, slot_sums], axis=1), 'rows', sp...]
    gather x9 -> x0, local copies, waits for them, and re-layouts: 5.87 us -> none  [the longest x3 2.28 us: apply_h(): far_vec = arrived[slot_of_ref]]
    all_gather x1 -> x0, blocking collectives: 5.78 us -> none  [shards(): column_piece = lax.all_gather(filtered, 'cols', axis=1, tiled=True)]
    all_to_all x4 -> x0, waiting for transfers between devices: 4.58 us -> none  [the longest x3 4.58 us: apply_h(): lax.all_to_all(jnp.concatenate([outgoing, slot_sums], axis=1), 'rows', sp...]
    unnamed x13 -> x9, local copies, waits for them, and re-layouts: 1.06 us -> 5.22 us
  transfers between devices with their start and end apart: 4 -> 0, of which waited for: 2 -> 0; matrix products, arithmetic and copies ran while one was open for 15% -> 0% of each run, Pallas kernels for 0% -> 0%
where the time goes in v2:
time: 69.5 us; the launch traced here: 69.2 us
  Pallas kernels  58.3 us (84%)
  local copies, waits for them, and re-layouts  6.73 us (10%)
  other arithmetic  2.82 us (4%)
  between operations  1.34 us (2%)
    pallas_call x1, Pallas kernels, fused_shards(): pl.pallas_call(functools.partial(filter_kernel, n_rows, n_cols), out_shap...  53.7 us
    unnamed x9, local copies, waits for them, and re-layouts  5.22 us
    pallas_call x1, Pallas kernels, pack_blocks(): pl.pallas_call(pack_kernel, grid_spec=pltpu.PrefetchScalarGridSpec(num_sc...  4.68 us

profile of v2, /device:TPU:0, one launch (start us, length us, event | category | flops | bytes accessed | tf_op | source)
XLA Modules:
  0.0 69.2 jit_solution(7405010512274468390)
XLA Ops:
  1.3 0.7 slice_subtract_fusion
  2.0 0.8 %negate_select_fusion = (s32[8,16]{1,0:T(8,128)S(1)}, s32[8,16]{1,0:T(8,128)S(1)}) fusion(s32[]{:T(128)S(6)} %axis_index.15, s32[8,24]{1,0:T(8,128)} %param.7), kind=kLoop, calls=%fused_computation.6 | loop fusion | flops 3200 | bytes 1540 | tf_op jit(solution)/shard_map/rem | solution.py:480
  2.8 0.4 fusion
  3.2 0.1 copy.12
  3.3 0.1 fusion.2
  3.4 0.8 %convert_add_fusion = s32[8,16]{1,0:T(8,128)S(1)} fusion(s32[8,16]{1,0:T(8,128)S(1)} %get-tuple-element.15, s32[8,16]{1,0:T(8,128)S(1)} %fusion.2, s32[8,24]{1,0:T(8,128)} %param.7), kind=kLoop, calls=%fused_computation.15 | loop fusion | flops 2944 | bytes 2048 | tf_op jit(solution)/shard_map/add | solution.py:485
  4.1 0.1 pad_add_fusion.index_ref
  4.2 0.1 broadcast_in_dim.44.lists_ref
  4.3 0.0 copy-start
  4.3 4.6 %copy-done = f32[8,24,128,128]{3,2,1,0:T(8,128)S(1)} copy-done((f32[8,24,128,128]{3,2,1,0:T(8,128)S(1)}, f32[8,24,128,128]{3,2,1,0:T(8,128)}, u32[]{:S(2)}) %copy-start) | copy-done | bytes 12582936
  8.9 0.0 copy-start.1
  8.9 0.0 copy-start.2
  8.9 0.0 copy-start.3
  8.9 4.7 %shard_map.85 = (bf16[1024,2816]{1,0:T(8,128)(2,1)S(1)}, bf16[1024,2816]{1,0:T(8,128)(2,1)S(1)}) custom-call(s32[8,24]{1,0:T(8,128)S(1)} %pad_add_fusion.index_ref, f32[8,24,128,128]{3,2,1,0:T(8,128)S(1)} %copy-done), custom_call_target="tpu_custom_call" | custom-call | tf_op jit(solution)/shard_map/pallas_call | solution.py:171
  13.6 0.0 copy-done.1
  13.6 0.0 copy-done.2
  13.6 0.0 copy-done.3
  13.6 53.7 %shard_map.86 = (f32[8,16,128]{2,1,0:T(8,128)S(1)}, f32[64,16]{1,0:T(8,128)S(1)}, f32[64,16]{1,0:T(8,128)S(1)}) custom-call(f32[1]{0:T(128)S(6)} %copy.16.center_ref, f32[8]{0:T(128)S(1)} %copy-done.2, f32[8]{0:T(128)S(1)} %copy-done.3, f32[8,16,128]{2,1,0:T(8,128)S(1)} %copy-done.1, s32[7,2,8,128]{3,2,1,0:T(8,128)S(1)} %broadcast_in_dim.44.lists_ref, ...), custom_call_target="tpu_custom_call" | custom-call | tf_op jit(solution)/shard_map/pallas_call | solution.py:497
  67.3 0.7 copy.13
  67.9 0.7 copy.14
  68.6 0.6 copy.17
  (2 shorter events, 0.0 us)
Async XLA Ops:
  4.3 4.6 %copy-start = (f32[8,24,128,128]{3,2,1,0:T(8,128)S(1)}, f32[8,24,128,128]{3,2,1,0:T(8,128)}, u32[]{:S(2)}) copy-start(f32[8,24,128,128]{3,2,1,0:T(8,128)} %blocks_ref.1) | copy-start | bytes 37748740
  8.9 4.7 %copy-start.1 = (f32[8,16,128]{2,1,0:T(8,128)S(1)}, f32[8,16,128]{2,1,0:T(8,128)}, u32[]{:S(2)}) copy-start(f32[8,16,128]{2,1,0:T(8,128)} %vec_ref.1) | copy-start | bytes 196612
  8.9 4.7 %copy-start.2 = (f32[8]{0:T(128)S(1)}, f32[8]{0:T(128)}, u32[]{:S(2)}) copy-start(f32[8]{0:T(128)} %shifts_ref.1) | copy-start | bytes 100
  8.9 4.7 %copy-start.3 = (f32[8]{0:T(128)S(1)}, f32[8]{0:T(128)}, u32[]{:S(2)}) copy-start(f32[8]{0:T(128)} %weights_ref.1) | copy-start | bytes 100

commit v3 on v2

--- a/solution.py
+++ b/solution.py
@@ -151,37 +151,93 @@
     return high, low
 
 
-def pack_kernel(index_ref, blocks_ref, high_ref, low_ref, acc):
-    row = pl.program_id(0)
-    width = blocks_ref.shape[-1]
-    acc[...] = jnp.zeros_like(acc)
-    for k in range(blocks_ref.shape[1]):
-        spot = index_ref[row, k]
-        acc[spot] = acc[spot] + blocks_ref[0, k]
-    for spot in range(acc.shape[0]):
-        high, low = split(acc[spot])
-        high_ref[:, spot * width : (spot + 1) * width] = high
-        low_ref[:, spot * width : (spot + 1) * width] = low
-
-
-def pack_blocks(index, hblocks, spots):
+def pack_kernel(
+    n_rows,
+    me_ref,
+    cols_ref,
+    blocks_hbm,
+    high_ref,
+    low_ref,
+    lists_ref,
+    blocks,
+    acc,
+    index,
+    scalars,
+    sem,
+    load_sems,
+):
+    width = blocks.shape[-1]
+    block_rows, per_row = cols_ref.shape
+    me = me_ref[0]
+
+    def load(row):
+        return pltpu.make_async_copy(blocks_hbm.at[row], blocks.at[row], load_sems.at[row])
+
+    for row in range(block_rows):
+        load(row).start()
+
+    def place_blocks():
+        columns = cols_ref[...].astype(jnp.float32)
+        place = lax.broadcasted_iota(jnp.int32, columns.shape, 1)
+        spots = columns - (me * block_rows).astype(jnp.float32)
+        for step in range(1, n_rows):
+            first = (lax.rem(me + step, n_rows) * block_rows).astype(jnp.float32)
+            inner = columns - first
+            hit = (place >= block_rows) & (inner >= 0.0) & (inner < block_rows)
+            low_row = jnp.where(hit, inner, float(block_rows))
+            low_row = jnp.min(jnp.min(low_row, axis=1, keepdims=True), axis=0, keepdims=True)
+            high_row = jnp.where(hit, inner, -1.0)
+            high_row = jnp.max(jnp.max(high_row, axis=1, keepdims=True), axis=0, keepdims=True)
+            slot = float(block_rows + CAP * (step - 1)) + jnp.where(inner == high_row, 1.0, 0.0)
+            spots = jnp.where(hit, slot, spots)
+            lists_ref[step - 1, 0:1, :] = jnp.broadcast_to(low_row, (1, width))
+            lists_ref[step - 1, 1:2, :] = jnp.broadcast_to(high_row, (1, width))
+        index[...] = jnp.zeros_like(index)
+        index[:, :per_row] = spots.astype(jnp.int32)
+        move = pltpu.make_async_copy(index, scalars, sem)
+        move.start()
+        move.wait()
+
+    place_blocks()
+
+    @pl.loop(0, block_rows)
+    def _(row):
+        acc[...] = jnp.zeros_like(acc)
+        load(row).wait()
+        for k in range(per_row):
+            spot = scalars[row, k]
+            acc[spot] = acc[spot] + blocks[row, k]
+        lines = pl.ds(pl.multiple_of(row * width, width), width)
+        for spot in range(acc.shape[0]):
+            high, low = split(acc[spot])
+            high_ref[lines, spot * width : (spot + 1) * width] = high
+            low_ref[lines, spot * width : (spot + 1) * width] = low
+
+
+def pack_blocks(n_rows, me, col_index, hblocks, spots):
     block_rows, per_row, width, _ = hblocks.shape
     out = jax.ShapeDtypeStruct((block_rows * width, spots * width), jnp.bfloat16)
-    out_spec = pl.BlockSpec((width, spots * width), lambda i, index_ref: (i, 0))
+    lists = (n_rows - 1, CAP, width)
+    vmem = pl.BlockSpec(memory_space=pltpu.VMEM)
     return pl.pallas_call(
-        pack_kernel,
-        grid_spec=pltpu.PrefetchScalarGridSpec(
-            num_scalar_prefetch=1,
-            grid=(block_rows,),
-            in_specs=[
-                pl.BlockSpec((1, per_row, width, width), lambda i, index_ref: (i, 0, 0, 0))
-            ],
-            out_specs=[out_spec, out_spec],
-            scratch_shapes=[pltpu.VMEM((spots, width, width), jnp.float32)],
-        ),
-        out_shape=[out, out],
-        compiler_params=pltpu.CompilerParams(vmem_limit_bytes=16 << 20),
-    )(index, hblocks)
+        functools.partial(pack_kernel, n_rows),
+        in_specs=[
+            pl.BlockSpec(memory_space=pltpu.SMEM),
+            vmem,
+            pl.BlockSpec(memory_space=pltpu.HBM),
+        ],
+        out_specs=[vmem, vmem, vmem],
+        scratch_shapes=[
+            pltpu.VMEM(hblocks.shape, jnp.float32),
+            pltpu.VMEM((spots, width, width), jnp.float32),
+            pltpu.VMEM((block_rows, 128), jnp.int32),
+            pltpu.SMEM((block_rows, 128), jnp.int32),
+            pltpu.SemaphoreType.DMA,
+            pltpu.SemaphoreType.DMA((block_rows,)),
+        ],
+        out_shape=[out, out, jax.ShapeDtypeStruct(lists, jnp.float32)],
+        compiler_params=pltpu.CompilerParams(vmem_limit_bytes=36 << 20),
+    )(me, col_index, hblocks)
 
 
 def filter_kernel(
@@ -192,16 +248,12 @@
     weights_ref,
     vec_ref,
     lists_ref,
-    high_hbm,
-    low_hbm,
+    high,
+    low,
     out_ref,
     gram_ref,
     ritz_ref,
-    high,
-    low,
     lists,
-    first_send,
-    first_recv,
     vec_send,
     vec_recv,
     prod_send,
@@ -209,18 +261,17 @@
     col_start,
     col_res,
     res_send,
-    energy_send,
-    energy_recv,
+    sums_send,
+    sums_recv,
     factor_send,
     factors,
     gram_send,
     gram_recv,
-    load_sem,
     list_sems,
     vec_sems,
     prod_sems,
     col_sems,
-    energy_sems,
+    sums_sems,
     gram_sems,
 ):
     block_rows, vecs, width = vec_ref.shape
@@ -231,13 +282,6 @@
     me_col = lax.axis_index("cols")
     pending = []
 
-    loads = [
-        pltpu.make_async_copy(high_hbm, high, load_sem.at[0]),
-        pltpu.make_async_copy(low_hbm, low, load_sem.at[1]),
-    ]
-    for load in loads:
-        load.start()
-
     barrier = pltpu.get_barrier_semaphore()
     for step in range(1, n_rows):
         pl.semaphore_signal(barrier, inc=1, device_id={"rows": lax.rem(me + step, n_rows)})
@@ -286,8 +330,7 @@
     start = flat(vec_ref)
 
     def named(step, slot, row):
-        mask = lists[step - 1, slot] == row
-        return jnp.concatenate([mask.astype(jnp.float32)] * (vecs // 8), axis=0) > 0.5
+        return jnp.broadcast_to(lists[step - 1, slot : slot + 1, :], (vecs, width)) == float(row)
 
     def dot(a, b, transposed):
         return lax.dot_general(
@@ -300,28 +343,62 @@
         count = top.shape[0]
         return wide_part[:count] + wide_part[count:] + dot(top, low[:, columns], transposed)
 
-    def apply_h(turn, vector, extra):
+    groups = vecs // 8
+    lane = lax.broadcasted_iota(jnp.int32, (8, width), 1)
+
+    def send_sums(turn, values):
+        packed = jnp.zeros((8, width), jnp.float32)
+        for q, value in enumerate(values):
+            for g in range(groups):
+                packed = jnp.where(lane == q * groups + g, value[g * 8 : (g + 1) * 8], packed)
+        sums_send[turn] = packed
+        return [
+            to_row(
+                sums_send.at[turn],
+                sums_recv.at[turn, peers - step],
+                sums_sems.at[turn],
+                step,
+            )
+            for step in range(1, n_rows)
+        ]
+
+    def total_sums(turn, copies, count):
+        arrive(copies)
+        total = sums_send[turn]
+        for step in range(1, n_rows):
+            total = total + sums_recv[turn, step - 1]
+        return [
+            jnp.concatenate(
+                [total[:, q * groups + g : q * groups + g + 1] for g in range(groups)], axis=0
+            )
+            for q in range(count)
+        ]
+
+    def send_vectors(turn, vector):
         copies = []
         for step in range(1, n_rows):
-            parts = []
             for slot in range(CAP):
                 picked = jnp.zeros((vecs, width), jnp.float32)
                 for row in range(block_rows):
                     piece = vector[:, row * width : (row + 1) * width]
                     picked = jnp.where(named(step, slot, row), piece, picked)
-                parts.append(picked)
-            if extra is None:
-                out, into = first_send.at[step - 1], first_recv.at[peers - step]
-            else:
-                parts.append(extra)
-                out, into = vec_send.at[turn - 1, step - 1], vec_recv.at[turn - 1, peers - step]
-            out[...] = jnp.concatenate(parts, axis=1)
-            copies.append(to_row(out, into, vec_sems.at[turn], step))
+                vec_send[turn, step - 1, :, slot * width : (slot + 1) * width] = picked
+            copies.append(
+                to_row(
+                    vec_send.at[turn, step - 1],
+                    vec_recv.at[turn, peers - step],
+                    vec_sems.at[turn],
+                    step,
+                )
+            )
+        return copies
+
+    def apply_h(turn, vector, sums, later):
+        if turn > 0:
+            copies = send_vectors(turn, vector)
+            sum_copies = send_sums(turn - 1, sums)
         top, bottom = split(vector)
         both = jnp.concatenate([top, bottom], axis=0)
-        if turn == 0:
-            for load in loads:
-                load.wait()
         products = []
         for step in range(1, n_rows):
             columns = slice(mine + (step - 1) * pair, mine + step * pair)
@@ -334,28 +411,28 @@
                     step,
                 )
             )
+        if turn == 0:
+            arrive(list_copies)
+            copies = send_vectors(turn, vector)
+            sum_copies = None
+        if later is not None:
+            col_copies.extend(later())
         near = slice(0, mine)
         result = times(both, top, near, False) + times(both, top, near, True)
-        arrive(copies)
-        source = first_recv if extra is None else vec_recv.at[turn - 1]
-        far = jnp.concatenate([source[step - 1, :, :pair] for step in range(1, n_rows)], axis=1)
-        total = extra
-        if extra is not None:
-            for step in range(1, n_rows):
-                total = total + source[step - 1, :, pair:]
-        top, bottom = split(far)
-        both = jnp.concatenate([top, bottom], axis=0)
-        result = result + times(both, top, slice(mine, mine + peers * pair), True)
-        arrive(products)
-        pieces = []
-        for row in range(block_rows):
-            piece = result[:, row * width : (row + 1) * width]
-            for step in range(1, n_rows):
-                for slot in range(CAP):
-                    back = prod_recv[turn, step - 1, :, slot * width : (slot + 1) * width]
-                    piece = piece + jnp.where(named(step, slot, row), back, 0.0)
-            pieces.append(piece)
-        return jnp.concatenate(pieces, axis=1), total
+        for step in range(1, n_rows):
+            copies[peers - step].wait_recv()
+            top, bottom = split(vec_recv[turn, step - 1])
+            both = jnp.concatenate([top, bottom], axis=0)
+            columns = slice(mine + (step - 1) * pair, mine + step * pair)
+            result = result + times(both, top, columns, True)
+        pieces = [result[:, row * width : (row + 1) * width] for row in range(block_rows)]
+        for step in range(1, n_rows):
+            products[peers - step].wait_recv()
+            for slot in range(CAP):
+                back = prod_recv[turn, step - 1, :, slot * width : (slot + 1) * width]
+                for row in range(block_rows):
+                    pieces[row] = pieces[row] + jnp.where(named(step, slot, row), back, 0.0)
+        return jnp.concatenate(pieces, axis=1), sum_copies
 
     def column_sum(value):
         return jnp.sum(value, axis=1, keepdims=True)
@@ -363,48 +440,45 @@
     center = center_ref[0]
     poles = [shifts_ref[m] for m in range(shifts_ref.shape[0])]
     base = functools.reduce(jnp.minimum, poles)
-    lane = lax.broadcasted_iota(jnp.int32, (vecs, width), 1)
     all_lanes = jnp.zeros((vecs, width), jnp.float32)
 
-    col_copies = [
-        to_col(vec_ref, col_start.at[me_col], col_sems.at[0], step) for step in range(1, n_cols)
-    ]
-    col_start[me_col] = vec_ref[...]
-    arrive(list_copies)
-    start_image, _ = apply_h(0, start, None)
+    col_copies = []
+
+    def send_start():
+        col_start[me_col] = vec_ref[...]
+        return [
+            to_col(vec_ref, col_start.at[me_col], col_sems.at[0], step)
+            for step in range(1, n_cols)
+        ]
+
+    def send_residual():
+        for row in range(block_rows):
+            res_send[row] = residual[:, row * width : (row + 1) * width]
+        col_res[me_col] = res_send[...]
+        return [
+            to_col(res_send, col_res.at[me_col], col_sems.at[1], step)
+            for step in range(1, n_cols)
+        ]
+
+    start_image, _ = apply_h(0, start, None, send_start)
     half_one = start_image - center * start
-    own_sums = jnp.where(lane == 0, column_sum(start * start), column_sum(half_one * half_one))
-    second, sums = apply_h(1, half_one, own_sums)
-    start_norm = sums[:, 0:1]
-    half_norm = sums[:, 1:2]
+    own_sums = [column_sum(start * start), column_sum(half_one * half_one)]
+    second, sum_copies = apply_h(1, half_one, own_sums, None)
+    start_norm, half_norm = total_sums(0, sum_copies, 2)
     alpha_one = start_norm / (half_norm + base * start_norm)
     op_image = second - center * half_one + base * start
     residual = start - alpha_one * op_image
-    for row in range(block_rows):
-        res_send[row] = residual[:, row * width : (row + 1) * width]
-    col_res[me_col] = res_send[...]
-    col_copies += [
-        to_col(res_send, col_res.at[me_col], col_sems.at[1], step) for step in range(1, n_cols)
-    ]
-    own_norm = column_sum(residual * residual) + all_lanes
-    residual_image, sums = apply_h(2, residual, own_norm)
-    res_norm = sums[:, 0:1]
+    own_norm = column_sum(residual * residual)
+    residual_image, sum_copies = apply_h(2, residual, [own_norm], send_residual)
+    (res_norm,) = total_sums(1, sum_copies, 1)
     beta = res_norm / start_norm
     direction = residual + beta * start
     half_two = residual_image - center * residual + beta * half_one
-    own_energy = column_sum(half_two * half_two + base * (direction * direction)) + all_lanes
-    energy_send[...] = own_energy
-    energy_copies = [
-        to_row(energy_send, energy_recv.at[peers - step], energy_sems, step)
-        for step in range(1, n_rows)
-    ]
-    arrive(energy_copies)
-    energy = own_energy
-    for step in range(1, n_rows):
-        energy = energy + energy_recv[step - 1]
+    own_energy = column_sum(half_two * half_two + base * (direction * direction))
+    (energy,) = total_sums(2, send_sums(2, [own_energy]), 1)
     alpha_one = alpha_one + all_lanes
     beta = beta + all_lanes
-    alpha_two = res_norm / energy
+    alpha_two = res_norm / energy + all_lanes
     from_start = all_lanes
     from_residual = all_lanes
     for m, pole in enumerate(poles):
@@ -423,7 +497,8 @@
             alpha_one * zeta_one + alpha_two * beta * zeta_one * zeta_two
         )
         from_residual = from_residual + weight * (alpha_two * zeta_two)
-    factor_send[...] = jnp.where(lane == 0, from_start, from_residual)
+    wide_lane = lax.broadcasted_iota(jnp.int32, (vecs, width), 1)
+    factor_send[...] = jnp.where(wide_lane == 0, from_start, from_residual)
     factors[me_col] = factor_send[...]
     col_copies += [
         to_col(factor_send, factors.at[me_col], col_sems.at[2], step)
@@ -457,10 +532,10 @@
     summed = gram_recv[0]
     for device in range(1, n_rows):
         summed = summed + gram_recv[device]
-    turned = jnp.transpose(summed * (1.0 / (n_rows * mine)))
+    scaled = summed * (1.0 / (n_rows * mine))
     columns = n_cols * vecs
-    gram_ref[...] = turned[:columns]
-    ritz_ref[...] = turned[columns:]
+    gram_ref[...] = scaled[:, :columns]
+    ritz_ref[...] = scaled[:, columns:]
     for copy in pending:
         copy.wait_send()
 
@@ -474,66 +549,48 @@
     spots = block_rows + CAP * peers
     mine = block_rows * width
     me = lax.axis_index("rows")
-    far = col_index[:, block_rows:]
-    owner = far // block_rows
-    row = far - owner * block_rows
-    ahead = lax.rem(owner - me + n_rows, n_rows)
-    hit = ahead[None] == jnp.arange(1, n_rows, dtype=jnp.int32)[:, None, None]
-    low_row = jnp.min(jnp.where(hit, row[None], block_rows), axis=(1, 2))
-    high_row = jnp.max(jnp.where(hit, row[None], -1), axis=(1, 2))
-    last = jnp.sum(jnp.where(hit, high_row[:, None, None], 0), axis=0)
-    slot = block_rows + CAP * (ahead - 1) + (row == last).astype(jnp.int32)
-    index = jnp.concatenate([col_index[:, :block_rows] - me * block_rows, slot], axis=1)
-    lists = jnp.broadcast_to(
-        jnp.stack([low_row, high_row], axis=1)[:, :, None, None], (peers, CAP, 8, width)
-    )
-    high, low = pack_blocks(index, hblocks, spots)
+    high, low, lists = pack_blocks(n_rows, me.reshape(1), col_index, hblocks, spots)
     columns = n_cols * vecs
     pair = CAP * width
     vmem = pl.BlockSpec(memory_space=pltpu.VMEM)
     smem = pl.BlockSpec(memory_space=pltpu.SMEM)
-    anywhere = pl.BlockSpec(memory_space=pl.ANY)
     f32 = jnp.float32
-    return pl.pallas_call(
+    filtered, gram, ritz = pl.pallas_call(
         functools.partial(filter_kernel, n_rows, n_cols),
         out_shape=[
             jax.ShapeDtypeStruct(right_side.shape, f32),
-            jax.ShapeDtypeStruct((columns, vecs), f32),
-            jax.ShapeDtypeStruct((columns, vecs), f32),
+            jax.ShapeDtypeStruct((vecs, columns), f32),
+            jax.ShapeDtypeStruct((vecs, columns), f32),
         ],
-        in_specs=[smem, smem, smem, vmem, vmem, anywhere, anywhere],
+        in_specs=[smem, smem, smem, vmem, vmem, vmem, vmem],
         out_specs=[vmem, vmem, vmem],
         scratch_shapes=[
-            pltpu.VMEM((mine, spots * width), jnp.bfloat16),
-            pltpu.VMEM((mine, spots * width), jnp.bfloat16),
-            pltpu.VMEM((peers, CAP, 8, width), jnp.int32),
-            pltpu.VMEM((peers, vecs, pair), f32),
-            pltpu.VMEM((peers, vecs, pair), f32),
-            pltpu.VMEM((2, peers, vecs, pair + width), f32),
-            pltpu.VMEM((2, peers, vecs, pair + width), f32),
+            pltpu.VMEM((peers, CAP, width), f32),
+            pltpu.VMEM((3, peers, vecs, pair), f32),
+            pltpu.VMEM((3, peers, vecs, pair), f32),
             pltpu.VMEM((3, peers, vecs, pair), f32),
             pltpu.VMEM((3, peers, vecs, pair), f32),
             pltpu.VMEM((n_cols,) + right_side.shape, f32),
             pltpu.VMEM((n_cols,) + right_side.shape, f32),
             pltpu.VMEM(right_side.shape, f32),
-            pltpu.VMEM((vecs, width), f32),
-            pltpu.VMEM((peers, vecs, width), f32),
+            pltpu.VMEM((3, 8, width), f32),
+            pltpu.VMEM((3, peers, 8, width), f32),
             pltpu.VMEM((vecs, width), f32),
             pltpu.VMEM((n_cols, vecs, width), f32),
             pltpu.VMEM((vecs, 2 * columns), f32),
             pltpu.VMEM((n_rows, vecs, 2 * columns), f32),
-            pltpu.SemaphoreType.DMA((2,)),
             pltpu.SemaphoreType.DMA((2, peers)),
             pltpu.SemaphoreType.DMA((3, 2, peers)),
             pltpu.SemaphoreType.DMA((3, 2, peers)),
             pltpu.SemaphoreType.DMA((3, 2, n_cols - 1)),
-            pltpu.SemaphoreType.DMA((2, peers)),
+            pltpu.SemaphoreType.DMA((3, 2, peers)),
             pltpu.SemaphoreType.DMA((2, peers)),
         ],
         compiler_params=pltpu.CompilerParams(
-            collective_id=0, has_side_effects=True, vmem_limit_bytes=40 << 20
+            collective_id=0, has_side_effects=True, vmem_limit_bytes=24 << 20
         ),
     )(center, shifts, filter_weights, right_side, lists, high, low)
+    return filtered, gram.T, ritz.T
 
 
 def solution(mesh):

time: 69.5 us -> 60.3 us (0.87)
  local copies, waits for them, and re-layouts: 6.73 us -> 2.52 us
  other arithmetic: 2.82 us -> 0 us
  Pallas kernels: 58.3 us -> 56.3 us
    pallas_call x1, Pallas kernels: 53.7 us -> 50.8 us  [fused_shards(): pl.pallas_call(functools.partial(filter_kernel, n_rows, n_cols), out_shap...]
    unnamed x9 -> x11, local copies, waits for them, and re-layouts: 5.22 us -> 2.52 us
    pallas_call x2 -> x0, local copies, waits for them, and re-layouts: 1.34 us -> none  [fused_shards(): pl.pallas_call(functools.partial(filter_kernel, n_rows, n_cols), out_shap...]
    pallas_call x1, Pallas kernels: 4.68 us -> 5.5 us  [pack_blocks(): pl.pallas_call(functools.partial(pack_kernel, n_rows), in_specs=[pl.Block...]
    add x2 -> x0, other arithmetic: 0.78 us -> none  [the longest x1 0.77 us: fused_shards(): slot = block_rows + CAP * (ahead - 1) + (row == last).astype(jnp.int32)]
    rem x1 -> x0, other arithmetic: 0.77 us -> none  [fused_shards(): ahead = lax.rem(owner - me + n_rows, n_rows)]
where the time goes in v3:
time: 60.3 us; the launch traced here: 60.1 us
  Pallas kernels  56.3 us (93%)
  local copies, waits for them, and re-layouts  2.52 us (4%)
  between operations  1.33 us (2%)
    pallas_call x1, Pallas kernels, fused_shards(): pl.pallas_call(functools.partial(filter_kernel, n_rows, n_cols), out_shap...  50.8 us
    pallas_call x1, Pallas kernels, pack_blocks(): pl.pallas_call(functools.partial(pack_kernel, n_rows), in_specs=[pl.Block...  5.5 us
    unnamed x11, local copies, waits for them, and re-layouts  2.52 us

profile of v3, /device:TPU:0, one launch (start us, length us, event | category | flops | bytes accessed | tf_op | source)
XLA Modules:
  0.0 60.1 jit_solution(5212239336623262396)
XLA Ops:
  1.3 0.0 copy-start.1
  1.3 0.7 %copy-done.1 = s32[8,24]{1,0:T(8,128)S(1)} copy-done((s32[8,24]{1,0:T(8,128)S(1)}, s32[8,24]{1,0:T(8,128)}, u32[]{:S(2)}) %copy-start.1) | copy-done | bytes 792
  2.0 0.0 copy-start
  2.0 0.0 copy-start.2
  2.0 0.0 copy-start.3
  2.0 5.5 %shard_map.85 = (bf16[1024,2816]{1,0:T(8,128)(2,1)S(1)}, bf16[1024,2816]{1,0:T(8,128)(2,1)S(1)}, f32[7,2,128]{2,1,0:T(2,128)S(1)}) custom-call(s32[1]{0:T(128)} %bitcast.me_ref, s32[8,24]{1,0:T(8,128)S(1)} %copy-done.1, f32[8,24,128,128]{3,2,1,0:T(8,128)} %blocks_hbm.1), custom_call_target="tpu_custom_call" | custom-call | tf_op jit(solution)/shard_map/pallas_call | solution.py:222
  7.5 0.0 copy-done
  7.5 0.0 copy-done.2
  7.5 0.0 copy-done.3
  7.5 50.8 %shard_map.86 = (f32[8,16,128]{2,1,0:T(8,128)S(1)}, f32[16,64]{1,0:T(8,128)S(1)}, f32[16,64]{1,0:T(8,128)S(1)}) custom-call(f32[1]{0:T(128)S(6)} %copy.12.center_ref, f32[8]{0:T(128)S(1)} %copy-done.2, f32[8]{0:T(128)S(1)} %copy-done.3, f32[8,16,128]{2,1,0:T(8,128)S(1)} %copy-done, f32[7,2,128]{2,1,0:T(2,128)S(1)} %get-tuple-element.9.lists_ref, ...), custom_call_target="tpu_custom_call" | custom-call | tf_op jit(solution)/shard_map/pallas_call | solution.py:558
  58.3 0.6 %copy.13 = f32[8,16,128]{2,1,0:T(8,128)} copy(f32[8,16,128]{2,1,0:T(8,128)S(1)} %get-tuple-element.18) | data formatting | bytes 131072
  59.0 0.6 copy.14
  59.6 0.6 copy.15
Async XLA Ops:
  1.3 0.7 %copy-start.1 = (s32[8,24]{1,0:T(8,128)S(1)}, s32[8,24]{1,0:T(8,128)}, u32[]{:S(2)}) copy-start(s32[8,24]{1,0:T(8,128)} %cols_ref.1) | copy-start | bytes 2308
  2.0 5.5 %copy-start = (f32[8,16,128]{2,1,0:T(8,128)S(1)}, f32[8,16,128]{2,1,0:T(8,128)}, u32[]{:S(2)}) copy-start(f32[8,16,128]{2,1,0:T(8,128)} %vec_ref.1) | copy-start | bytes 196612
  2.0 5.5 %copy-start.2 = (f32[8]{0:T(128)S(1)}, f32[8]{0:T(128)}, u32[]{:S(2)}) copy-start(f32[8]{0:T(128)} %shifts_ref.1) | copy-start | bytes 100
  2.0 5.5 %copy-start.3 = (f32[8]{0:T(128)S(1)}, f32[8]{0:T(128)}, u32[]{:S(2)}) copy-start(f32[8]{0:T(128)} %weights_ref.1) | copy-start | bytes 100
